TPU v7x, 128 devices: a whole 4x4x4 slice. The times are simulated.
128 devices in a mesh: colour: 2 (over core), sub: 64 (over z, y, x).
Axes of the slice: x: 4, y: 4, z: 4, core: 2. Of those that a mesh axis runs over, the one named last changes fastest.
Arguments:
- rhs: float32 [3, 256, 256, 512], P(None, 'sub'), may hold values from -60 to 60
- diagonal: float32 [256, 256, 512], P('sub'), may hold values from 0.2 to 6
Outputs:
- solution: float32 [3, 256, 256, 512], P(None, 'sub', None, 'colour')
- residual: float32 [3, 256, 256, 512], P(None, 'sub', None, 'colour')
- norms: float32 [3], replicated
All inputs are finite; a program needn't handle non-finite values.
Results may differ from a plain program's by a relative error of at most 0.0003.
Values sent between devices are 32-bit elements; how exact they have to be, the bound alone decides.
No kernel may reach another device: no remote copies, remote signals or barrier semaphores. Data moves between devices by JAX's collectives and lax.ppermute only.
A program may use at most 128 MiB of HBM per device.

v0:
```python
import jax
import jax.numpy as jnp
from jax import lax
from jax.sharding import Mesh
from jax.sharding import PartitionSpec as P

CX = 4
NY = 256
NZ = 512
RIM = 1
SWEEPS = 8
BATCH = 1
MICRO = 3
SUB = ("sub_0", "sub_1", "sub_2")
COLOUR_SUB = ("colour", "sub_0", "sub_1", "sub_2")


OMEGA = 0.8


def extended_2(block, sides, width):
    for axis, dim in sides:
        count = lax.axis_size(axis)
        forward = [(i, i + 1) for i in range(count - 1)]
        backward = [(target, source) for source, target in forward]
        low = lax.ppermute(
            lax.slice_in_dim(block, block.shape[dim] - width, None, axis=dim), axis, forward
        )
        high = lax.ppermute(lax.slice_in_dim(block, 0, width, axis=dim), axis, backward)
        block = jnp.concatenate([low, block, high], axis=dim)
    return block


def from_everyone(shard, axis):
    copies = jnp.broadcast_to(shard, (lax.axis_size(axis), *shard.shape))
    return lax.all_to_all(copies, axis, split_axis=0, concat_axis=0, tiled=True)


def of_everyone(shard, axis):
    return from_everyone(shard, axis).sum(axis=0)


def in_one(arrays, axis):
    vector, at, finished = (jnp.concatenate([a.reshape(-1) for a in arrays]), 0, [])
    so_far = of_everyone(vector, axis)
    for a in arrays:
        finished.append(so_far[at : at + a.size].reshape(a.shape))
        at += a.size
    return tuple(finished)


def swapped(value, axis, apart):
    mask = 2**apart
    pairs = [(source, source ^ mask) for source in range(lax.axis_size(axis))]
    return lax.ppermute(value, axis, pairs)


def by_axis(shard, axes):
    for axis in axes:
        shard = lax.psum(shard, axis)
    return shard


def bordered(extended, xpad, zpad):
    padded = jnp.pad(extended, ((0, 0), (xpad, xpad), (1, 1), (zpad, zpad)))
    beside = padded[:, 2:, 1:-1, 1:-1] + padded[:, :-2, 1:-1, 1:-1]
    beside = beside + padded[:, 1:-1, 2:, 1:-1] + padded[:, 1:-1, :-2, 1:-1]
    beside = beside + padded[:, 1:-1, 1:-1, 2:] + padded[:, 1:-1, 1:-1, :-2]
    return beside


def jacobi(resid, diag, mask):
    scale = OMEGA / (6.0 + diag)
    found = jnp.zeros_like(resid)
    for sweep in range(SWEEPS):
        beside = bordered(found, 1, 1)
        found = (found + scale * (resid - (6.0 + diag) * found + beside)) * mask
    return found


def slab_operator(field, diagonal):
    extended = extended_2(field, ((SUB, 1),), 1)
    sides = bordered(extended, 0, 1)
    return (6.0 + diagonal) * field - sides


def colour_step(current, resid, diagonal, diag_rim, colour, device, total):
    half = CX // 2
    span = half + 2 * RIM
    offset = colour * half
    padded_resid = extended_2(resid, ((SUB, 1),), RIM)
    region_resid = lax.dynamic_slice_in_dim(padded_resid, offset, span, 1)
    region_diag = lax.dynamic_slice_in_dim(diag_rim, offset, span, 0)
    place = device * CX + offset - RIM + lax.iota(jnp.int32, span)
    mask = ((place >= 0) & (place < total)).astype(jnp.float32)[:, None, None]
    found = jacobi(region_resid * mask, region_diag, mask)
    placed = jnp.zeros((resid.shape[0], CX + 2 * RIM, resid.shape[2], resid.shape[3]), jnp.float32)
    placed = lax.dynamic_update_slice_in_dim(placed, found, offset, 1)
    outgoing = jnp.concatenate([placed[:, :RIM], placed[:, CX + RIM :]], axis=1)
    arrived = extended_2(outgoing, ((SUB, 1),), RIM)
    from_left = jnp.pad(arrived[:, :RIM], ((0, 0), (0, CX - RIM), (0, 0), (0, 0)))
    from_right = jnp.pad(arrived[:, 3 * RIM :], ((0, 0), (CX - RIM, 0), (0, 0), (0, 0)))
    correction = placed[:, RIM : RIM + CX] + from_left + from_right
    image = slab_operator(correction, diagonal)
    upper_part = jnp.sum(resid * correction, axis=(1, 2, 3))
    lower_part = jnp.sum(correction * image, axis=(1, 2, 3))
    upper, lower = in_one((upper_part, lower_part), SUB)
    alpha = (upper / lower)[:, None, None, None]
    return (current + alpha * correction, resid - alpha * image)


def shards(rhs, diagonal):
    colour = lax.axis_index("colour")
    device = lax.axis_index(SUB)
    total = lax.axis_size(SUB) * CX
    diag_rim = extended_2(diagonal, ((SUB, 0),), RIM)
    half_z = NZ // 2
    lower_z = colour * half_z
    sol_parts = []
    res_parts = []
    blank = jnp.zeros((BATCH, CX, NY, NZ), jnp.float32)
    carry_u = blank
    carry_r = rhs[:BATCH]
    first = colour == 0
    for step in range(MICRO + 1):
        section_batch = jnp.clip(step - colour, 0, MICRO - 1)
        source = lax.dynamic_slice_in_dim(rhs, section_batch * BATCH, BATCH, 0)
        current = jnp.where(first, blank, carry_u)
        resid = jnp.where(first, source, carry_r)
        new_u, new_r = colour_step(current, resid, diagonal, diag_rim, colour, device, total)
        got_u, got_r = swapped((new_u, new_r), "colour", 0)
        carry_u = got_u
        carry_r = got_r
        if step >= 1:
            done_u = jnp.where(first, got_u, new_u)
            done_r = jnp.where(first, got_r, new_r)
            part_u = lax.dynamic_slice_in_dim(done_u, lower_z, half_z, 3)
            part_r = lax.dynamic_slice_in_dim(done_r, lower_z, half_z, 3)
            sol_parts.append(part_u)
            res_parts.append(part_r)
    solution = jnp.concatenate(sol_parts, axis=0)
    residual = jnp.concatenate(res_parts, axis=0)
    squares = by_axis(jnp.sum(residual * residual, axis=(1, 2, 3)), COLOUR_SUB)
    return (solution, residual, jnp.sqrt(squares))


def solution(mesh):
    torus = Mesh(
        mesh.devices.reshape(mesh.shape["colour"], 4, 4, 4), ("colour", "sub_0", "sub_1", "sub_2")
    )
    return jax.shard_map(
        shards,
        mesh=torus,
        in_specs=(P(None, SUB, None, None), P(SUB, None, None)),
        out_specs=(P(None, SUB, None, "colour"), P(None, SUB, None, "colour"), P()),
        check_vma=False,
    )
```

profile of v0, /device:TPU:0, one launch (start us, length us, event | category | flops | bytes accessed | tf_op | source)
XLA Modules:
  0.0 553.9 jit_solution(10662957906198347244)
XLA Ops:
  1.9 4.3 collective-permute-start
  11.4 5.4 collective-permute-start.2
  18.1 4.4 collective-permute-done.1
  22.5 5.4 collective-permute-done.2
  27.9 4.9 collective-permute-done.3
  33.1 4.9 fusion.321
  59.5 8.2 %collective-permute-done.4 = f32[1,1,256,512]{3,2,1,0:T(8,128)S(1)} collective-permute-done((f32[1,1,256,512]{3,2,1,0:T(8,128)S(1)}, f32[1,1,256,512]{3,2,1,0:T(8,128)S(1)}, u32[]{:S(2)}, u32[]{:S(2)}) %collective-permute-start.4) | collective-permute-done | bytes 524320 | tf_op jit(solution)/shard_map/ppermute | solution.py:26
  67.7 4.4 collective-permute-done.5
  72.6 4.7 collective-permute-start.7
  79.2 6.4 %collective-permute-done.7 = f32[1,1,256,512]{3,2,1,0:T(8,128)S(1)} collective-permute-done((f32[1,1,256,512]{3,2,1,0:T(8,128)S(1)}, f32[1,1,256,512]{3,2,1,0:T(8,128)S(1)}, u32[]{:S(2)}, u32[]{:S(2)}) %collective-permute-start.7) | collective-permute-done | bytes 524320 | tf_op jit(solution)/shard_map/ppermute | solution.py:26
  85.6 4.3 collective-permute-done.6
  92.3 4.0 multiply_reduce_fusion.8
  97.6 30.6 %all_to_all.24 = f32[64,1,2]{2,1,0:T(1,128)S(1)} all-to-all(f32[64,1,2]{2,1,0:T(1,128)S(1)} %broadcast_in_dim.17), channel_id=1, replica_groups=mesh['colour'=2,'sub_0'=4,'sub_1'=4,'sub_2'=4] {'sub_0','sub_1','sub_2'}, dimensions={0} | all-to-all | bytes 1024 | tf_op jit(solution)/shard_map/all_to_all | solution.py:36
  130.2 5.0 multiply_subtract_fusion.3
  135.2 4.5 collective-permute-done.9
  145.9 10.8 %collective-permute-done.10 = f32[1,1,256,512]{3,2,1,0:T(8,128)S(1)} collective-permute-done((f32[1,1,256,512]{3,2,1,0:T(8,128)S(1)}, f32[1,1,256,512]{3,2,1,0:T(8,128)S(1)}, u32[]{:S(2)}, u32[]{:S(2)}) %collective-permute-start.10) | collective-permute-done | bytes 524320 | tf_op jit(solution)/shard_map/ppermute | solution.py:26
  156.7 4.1 collective-permute-done.11
  184.2 9.7 %collective-permute-done.12 = f32[1,1,256,512]{3,2,1,0:T(8,128)S(1)} collective-permute-done((f32[1,1,256,512]{3,2,1,0:T(8,128)S(1)}, f32[1,1,256,512]{3,2,1,0:T(8,128)S(1)}, u32[]{:S(2)}, u32[]{:S(2)}) %collective-permute-start.12) | collective-permute-done | bytes 524320 | tf_op jit(solution)/shard_map/ppermute | solution.py:26
  193.9 4.5 collective-permute-done.13
  199.4 5.6 %collective-permute-start.15 = (f32[1,1,256,512]{3,2,1,0:T(8,128)S(1)}, f32[1,1,256,512]{3,2,1,0:T(8,128)S(1)}, u32[]{:S(2)}, u32[]{:S(2)}) collective-permute-start(f32[1,1,256,512]{3,2,1,0:T(8,128)S(1)} %get-tuple-element.42), channel_id=1, source_target_pairs={{0,1},{1,2},{2,3},{3,4},{4,5},{5,6},{6,7},{7,8},{8,9},{9,10},{10,1... | collective-permute-start | bytes 1572872 | tf_op jit(solution)/shard_map/ppermute | solution.py:26
  206.6 8.5 %collective-permute-done.15 = f32[1,1,256,512]{3,2,1,0:T(8,128)S(1)} collective-permute-done((f32[1,1,256,512]{3,2,1,0:T(8,128)S(1)}, f32[1,1,256,512]{3,2,1,0:T(8,128)S(1)}, u32[]{:S(2)}, u32[]{:S(2)}) %collective-permute-start.15) | collective-permute-done | bytes 524320 | tf_op jit(solution)/shard_map/ppermute | solution.py:26
  215.0 4.3 collective-permute-done.14
  221.6 3.8 multiply_reduce_fusion.6
  226.6 26.4 %all_to_all.25 = f32[64,1,2]{2,1,0:T(1,128)S(1)} all-to-all(f32[64,1,2]{2,1,0:T(1,128)S(1)} %broadcast_in_dim.18), channel_id=1, replica_groups=mesh['colour'=2,'sub_0'=4,'sub_1'=4,'sub_2'=4] {'sub_0','sub_1','sub_2'}, dimensions={0} | all-to-all | bytes 1024 | tf_op jit(solution)/shard_map/all_to_all | solution.py:36
  254.9 4.0 multiply_subtract_fusion.2
  258.9 4.5 collective-permute-done.17
  269.7 10.8 %collective-permute-done.18 = f32[1,1,256,512]{3,2,1,0:T(8,128)S(1)} collective-permute-done((f32[1,1,256,512]{3,2,1,0:T(8,128)S(1)}, f32[1,1,256,512]{3,2,1,0:T(8,128)S(1)}, u32[]{:S(2)}, u32[]{:S(2)}) %collective-permute-start.18) | collective-permute-done | bytes 524320 | tf_op jit(solution)/shard_map/ppermute | solution.py:26
  280.4 4.1 collective-permute-done.19
  308.0 9.7 %collective-permute-done.20 = f32[1,1,256,512]{3,2,1,0:T(8,128)S(1)} collective-permute-done((f32[1,1,256,512]{3,2,1,0:T(8,128)S(1)}, f32[1,1,256,512]{3,2,1,0:T(8,128)S(1)}, u32[]{:S(2)}, u32[]{:S(2)}) %collective-permute-start.20) | collective-permute-done | bytes 524320 | tf_op jit(solution)/shard_map/ppermute | solution.py:26
  317.6 4.5 collective-permute-done.21
  323.1 5.6 %collective-permute-start.23 = (f32[1,1,256,512]{3,2,1,0:T(8,128)S(1)}, f32[1,1,256,512]{3,2,1,0:T(8,128)S(1)}, u32[]{:S(2)}, u32[]{:S(2)}) collective-permute-start(f32[1,1,256,512]{3,2,1,0:T(8,128)S(1)} %get-tuple-element.38), channel_id=1, source_target_pairs={{0,1},{1,2},{2,3},{3,4},{4,5},{5,6},{6,7},{7,8},{8,9},{9,10},{10,1... | collective-permute-start | bytes 1572872 | tf_op jit(solution)/shard_map/ppermute | solution.py:26
  330.3 8.4 %collective-permute-done.23 = f32[1,1,256,512]{3,2,1,0:T(8,128)S(1)} collective-permute-done((f32[1,1,256,512]{3,2,1,0:T(8,128)S(1)}, f32[1,1,256,512]{3,2,1,0:T(8,128)S(1)}, u32[]{:S(2)}, u32[]{:S(2)}) %collective-permute-start.23) | collective-permute-done | bytes 524320 | tf_op jit(solution)/shard_map/ppermute | solution.py:26
  338.7 4.3 collective-permute-done.22
  345.3 3.9 multiply_reduce_fusion.4
  350.6 26.4 %all_to_all.26 = f32[64,1,2]{2,1,0:T(1,128)S(1)} all-to-all(f32[64,1,2]{2,1,0:T(1,128)S(1)} %broadcast_in_dim.19), channel_id=1, replica_groups=mesh['colour'=2,'sub_0'=4,'sub_1'=4,'sub_2'=4] {'sub_0','sub_1','sub_2'}, dimensions={0} | all-to-all | bytes 1024 | tf_op jit(solution)/shard_map/all_to_all | solution.py:36
  379.1 4.2 multiply_subtract_fusion.1
  397.6 7.3 %collective-permute-done.26 = f32[1,1,256,512]{3,2,1,0:T(8,128)S(1)} collective-permute-done((f32[1,1,256,512]{3,2,1,0:T(8,128)S(1)}, f32[1,1,256,512]{3,2,1,0:T(8,128)S(1)}, u32[]{:S(2)}, u32[]{:S(2)}) %collective-permute-start.26) | collective-permute-done | bytes 524320 | tf_op jit(solution)/shard_map/ppermute | solution.py:26
  405.0 4.3 collective-permute-done.27
  432.7 9.7 %collective-permute-done.28 = f32[1,1,256,512]{3,2,1,0:T(8,128)S(1)} collective-permute-done((f32[1,1,256,512]{3,2,1,0:T(8,128)S(1)}, f32[1,1,256,512]{3,2,1,0:T(8,128)S(1)}, u32[]{:S(2)}, u32[]{:S(2)}) %collective-permute-start.28) | collective-permute-done | bytes 524320 | tf_op jit(solution)/shard_map/ppermute | solution.py:26
  442.4 4.5 collective-permute-done.29
  447.3 5.8 %collective-permute-start.31 = (f32[1,1,256,512]{3,2,1,0:T(8,128)S(1)}, f32[1,1,256,512]{3,2,1,0:T(8,128)S(1)}, u32[]{:S(2)}, u32[]{:S(2)}) collective-permute-start(f32[1,1,256,512]{3,2,1,0:T(8,128)S(1)} %get-tuple-element.34), channel_id=1, source_target_pairs={{0,1},{1,2},{2,3},{3,4},{4,5},{5,6},{6,7},{7,8},{8,9},{9,10},{10,1... | collective-permute-start | bytes 1572872 | tf_op jit(solution)/shard_map/ppermute | solution.py:26
  456.7 6.6 %collective-permute-done.31 = f32[1,1,256,512]{3,2,1,0:T(8,128)S(1)} collective-permute-done((f32[1,1,256,512]{3,2,1,0:T(8,128)S(1)}, f32[1,1,256,512]{3,2,1,0:T(8,128)S(1)}, u32[]{:S(2)}, u32[]{:S(2)}) %collective-permute-start.31) | collective-permute-done | bytes 524320 | tf_op jit(solution)/shard_map/ppermute | solution.py:26
  463.2 4.1 collective-permute-done.30
  469.7 3.8 multiply_reduce_fusion.2
  474.9 26.4 %all_to_all.27 = f32[64,1,2]{2,1,0:T(1,128)S(1)} all-to-all(f32[64,1,2]{2,1,0:T(1,128)S(1)} %broadcast_in_dim.20), channel_id=1, replica_groups=mesh['colour'=2,'sub_0'=4,'sub_1'=4,'sub_2'=4] {'sub_0','sub_1','sub_2'}, dimensions={0} | all-to-all | bytes 1024 | tf_op jit(solution)/shard_map/all_to_all | solution.py:36
  519.8 8.7 %psum.29 = f32[3]{0:T(128)S(1)} all-reduce(f32[3]{0:T(128)S(1)} %psum.28), channel_id=1, replica_groups=mesh['colour'=2,'sub_0'=4,'sub_1'=4,'sub_2'=4] {'sub_0'}, use_global_device_ids=true, to_apply=%region_14.15 | all-reduce | flops 3 | bytes 24 | tf_op jit(solution)/shard_map/psum | solution.py:60
  529.8 8.9 %psum.30 = f32[3]{0:T(128)S(1)} all-reduce(f32[3]{0:T(128)S(1)} %psum.29), channel_id=1, replica_groups=mesh['colour'=2,'sub_0'=4,'sub_1'=4,'sub_2'=4] {'sub_1'}, use_global_device_ids=true, to_apply=%region_15.16 | all-reduce | flops 3 | bytes 24 | tf_op jit(solution)/shard_map/psum | solution.py:60
  540.5 9.1 %psum.31 = f32[3]{0:T(128)S(1)} all-reduce(f32[3]{0:T(128)S(1)} %psum.30), channel_id=1, replica_groups=mesh['colour'=2,'sub_0'=4,'sub_1'=4,'sub_2'=4] {'sub_2'}, use_global_device_ids=true, to_apply=%region_16.17 | all-reduce | flops 3 | bytes 24 | tf_op jit(solution)/shard_map/psum | solution.py:60
  (195 shorter events, 178.0 us)
Async XLA Ops:
  1.9 16.2 %collective-permute-start = (f32[1,256,512]{2,1,0:T(8,128)S(1)}, f32[1,256,512]{2,1,0:T(8,128)}, u32[]{:S(2)}, u32[]{:S(2)}) collective-permute-start(f32[1,256,512]{2,1,0:T(8,128)S(1)} %get-tuple-element.50), channel_id=1, source_target_pairs={{0,1},{1,2},{2,3},{3,4},{4,5},{5,6},{6,7},{7,8},{8,9},{9,10},{10,1... | collective-permute-start | bytes 1572872 | tf_op jit(solution)/shard_map/ppermute | solution.py:26
  6.2 16.3 %collective-permute-start.1 = (f32[1,256,512]{2,1,0:T(8,128)S(1)}, f32[1,256,512]{2,1,0:T(8,128)}, u32[]{:S(2)}, u32[]{:S(2)}) collective-permute-start(f32[1,256,512]{2,1,0:T(8,128)S(1)} %get-tuple-element.51), channel_id=1, source_target_pairs={{1,0},{2,1},{3,2},{4,3},{5,4},{6,5},{7,6},{8,7},{9,8},{10,9},{11,1... | collective-permute-start | bytes 1572872 | tf_op jit(solution)/shard_map/ppermute | solution.py:29
  10.3 22.5 %copy-start.19 = (f32[1,4,256,512]{3,2,1,0:T(8,128)}, f32[1,4,256,512]{3,2,1,0:T(8,128)S(1)}, u32[]{:S(2)}) copy-start(f32[1,4,256,512]{3,2,1,0:T(8,128)S(1)} %slice_select_fusion) | copy-start | bytes 6291460
  11.4 16.5 %collective-permute-start.2 = (f32[1,1,256,512]{3,2,1,0:T(8,128)}, f32[1,1,256,512]{3,2,1,0:T(8,128)}, u32[]{:S(2)}, u32[]{:S(2)}) collective-permute-start(f32[1,1,256,512]{3,2,1,0:T(8,128)} %get-tuple-element.48), channel_id=1, source_target_pairs={{0,1},{1,2},{2,3},{3,4},{4,5},{5,6},{6,7},{7,8},{8,9},{9,10},{10,1... | collective-permute-start | bytes 1572872 | tf_op jit(solution)/shard_map/ppermute | solution.py:26
  16.8 16.0 %collective-permute-start.3 = (f32[1,1,256,512]{3,2,1,0:T(8,128)}, f32[1,1,256,512]{3,2,1,0:T(8,128)}, u32[]{:S(2)}, u32[]{:S(2)}) collective-permute-start(f32[1,1,256,512]{3,2,1,0:T(8,128)} %get-tuple-element.49), channel_id=1, source_target_pairs={{1,0},{2,1},{3,2},{4,3},{5,4},{6,5},{7,6},{8,7},{9,8},{10,9},{11,1... | collective-permute-start | bytes 1572872 | tf_op jit(solution)/shard_map/ppermute | solution.py:29
  52.8 39.4 %slice-start = ((s8[6291456]{0:T(1024)(128)(4,1)}), s8[2097152]{0:T(1024)(128)(4,1)S(1)}, s32[]{:S(2)}) async-start(s8[6291456]{0:T(1024)(128)(4,1)} %bitcast.232), calls=%async_computation.4 | async-start | bytes 4194304
  55.2 17.3 %copy-start.11 = (f32[1,6,256,512]{3,2,1,0:T(8,128)}, f32[1,6,256,512]{3,2,1,0:T(8,128)S(1)}, u32[]{:S(2)}) copy-start(f32[1,6,256,512]{3,2,1,0:T(8,128)S(1)} %fusion.81) | copy-start | bytes 9437188
  55.3 12.4 %collective-permute-start.4 = (f32[1,1,256,512]{3,2,1,0:T(8,128)S(1)}, f32[1,1,256,512]{3,2,1,0:T(8,128)S(1)}, u32[]{:S(2)}, u32[]{:S(2)}) collective-permute-start(f32[1,1,256,512]{3,2,1,0:T(8,128)S(1)} %get-tuple-element.32), channel_id=1, source_target_pairs={{0,1},{1,2},{2,3},{3,4},{4,5},{5,6},{6,7},{7,8},{8,9},{9,10},{10,1... | collective-permute-start | bytes 1572872 | tf_op jit(solution)/shard_map/ppermute | solution.py:26
  57.9 34.3 %slice-start.1 = ((s8[6291456]{0:T(1024)(128)(4,1)}), s8[4194304]{0:T(1024)(128)(4,1)S(1)}, s32[]{:S(2)}) async-start(s8[6291456]{0:T(1024)(128)(4,1)} %bitcast.232), calls=%async_computation.5 | async-start | bytes 8388608
  57.9 14.2 %collective-permute-start.5 = (f32[1,1,256,512]{3,2,1,0:T(8,128)S(1)}, f32[1,1,256,512]{3,2,1,0:T(8,128)S(1)}, u32[]{:S(2)}, u32[]{:S(2)}) collective-permute-start(f32[1,1,256,512]{3,2,1,0:T(8,128)S(1)} %get-tuple-element.33), channel_id=1, source_target_pairs={{1,0},{2,1},{3,2},{4,3},{5,4},{6,5},{7,6},{8,7},{9,8},{10,9},{11,1... | collective-permute-start | bytes 1572872 | tf_op jit(solution)/shard_map/ppermute | solution.py:29
  72.6 13.0 %collective-permute-start.7 = (f32[1,1,256,512]{3,2,1,0:T(8,128)S(1)}, f32[1,1,256,512]{3,2,1,0:T(8,128)S(1)}, u32[]{:S(2)}, u32[]{:S(2)}) collective-permute-start(f32[1,1,256,512]{3,2,1,0:T(8,128)S(1)} %get-tuple-element.46), channel_id=1, source_target_pairs={{0,1},{1,2},{2,3},{3,4},{4,5},{5,6},{6,7},{7,8},{8,9},{9,10},{10,1... | collective-permute-start | bytes 1572872 | tf_op jit(solution)/shard_map/ppermute | solution.py:26
  77.3 12.6 %collective-permute-start.6 = (f32[1,1,256,512]{3,2,1,0:T(8,128)S(1)}, f32[1,1,256,512]{3,2,1,0:T(8,128)S(1)}, u32[]{:S(2)}, u32[]{:S(2)}) collective-permute-start(f32[1,1,256,512]{3,2,1,0:T(8,128)S(1)} %get-tuple-element.47), channel_id=1, source_target_pairs={{1,0},{2,1},{3,2},{4,3},{5,4},{6,5},{7,6},{8,7},{9,8},{10,9},{11,1... | collective-permute-start | bytes 1572872 | tf_op jit(solution)/shard_map/ppermute | solution.py:29
  135.2 4.5 collective-permute-start.9
  141.8 79.8 %copy-start.9 = (f32[1,4,256,512]{3,2,1,0:T(8,128)}, f32[1,4,256,512]{3,2,1,0:T(8,128)S(1)}, u32[]{:S(2)}) copy-start(f32[1,4,256,512]{3,2,1,0:T(8,128)S(1)} %dynamic-slice_select_fusion.2) | copy-start | bytes 6291460
  141.8 19.1 %copy-start.5 = (f32[1,4,256,512]{3,2,1,0:T(8,128)S(1)}, f32[1,4,256,512]{3,2,1,0:T(8,128)}, u32[]{:S(2)}) copy-start(f32[1,4,256,512]{3,2,1,0:T(8,128)} %copy-done.4) | copy-start | bytes 6291460
  141.9 14.8 %collective-permute-start.10 = (f32[1,1,256,512]{3,2,1,0:T(8,128)S(1)}, f32[1,1,256,512]{3,2,1,0:T(8,128)S(1)}, u32[]{:S(2)}, u32[]{:S(2)}) collective-permute-start(f32[1,1,256,512]{3,2,1,0:T(8,128)S(1)} %get-tuple-element.44), channel_id=1, source_target_pairs={{0,1},{1,2},{2,3},{3,4},{4,5},{5,6},{6,7},{7,8},{8,9},{9,10},{10,1... | collective-permute-start | bytes 1572872 | tf_op jit(solution)/shard_map/ppermute | solution.py:26
  144.6 16.2 %collective-permute-start.11 = (f32[1,1,256,512]{3,2,1,0:T(8,128)S(1)}, f32[1,1,256,512]{3,2,1,0:T(8,128)S(1)}, u32[]{:S(2)}, u32[]{:S(2)}) collective-permute-start(f32[1,1,256,512]{3,2,1,0:T(8,128)S(1)} %get-tuple-element.45), channel_id=1, source_target_pairs={{1,0},{2,1},{3,2},{4,3},{5,4},{6,5},{7,6},{8,7},{9,8},{10,9},{11,1... | collective-permute-start | bytes 1572872 | tf_op jit(solution)/shard_map/ppermute | solution.py:29
  180.4 18.4 %copy-start.15 = (f32[1,6,256,512]{3,2,1,0:T(8,128)}, f32[1,6,256,512]{3,2,1,0:T(8,128)S(1)}, u32[]{:S(2)}) copy-start(f32[1,6,256,512]{3,2,1,0:T(8,128)S(1)} %fusion.145) | copy-start | bytes 9437188
  180.5 13.4 %collective-permute-start.12 = (f32[1,1,256,512]{3,2,1,0:T(8,128)S(1)}, f32[1,1,256,512]{3,2,1,0:T(8,128)S(1)}, u32[]{:S(2)}, u32[]{:S(2)}) collective-permute-start(f32[1,1,256,512]{3,2,1,0:T(8,128)S(1)} %get-tuple-element.30), channel_id=1, source_target_pairs={{0,1},{1,2},{2,3},{3,4},{4,5},{5,6},{6,7},{7,8},{8,9},{9,10},{10,1... | collective-permute-start | bytes 1572872 | tf_op jit(solution)/shard_map/ppermute | solution.py:26
  182.9 15.5 %collective-permute-start.13 = (f32[1,1,256,512]{3,2,1,0:T(8,128)S(1)}, f32[1,1,256,512]{3,2,1,0:T(8,128)S(1)}, u32[]{:S(2)}, u32[]{:S(2)}) collective-permute-start(f32[1,1,256,512]{3,2,1,0:T(8,128)S(1)} %get-tuple-element.31), channel_id=1, source_target_pairs={{1,0},{2,1},{3,2},{4,3},{5,4},{6,5},{7,6},{8,7},{9,8},{10,9},{11,1... | collective-permute-start | bytes 1572872 | tf_op jit(solution)/shard_map/ppermute | solution.py:29
  199.4 15.7 %collective-permute-start.15 = (f32[1,1,256,512]{3,2,1,0:T(8,128)S(1)}, f32[1,1,256,512]{3,2,1,0:T(8,128)S(1)}, u32[]{:S(2)}, u32[]{:S(2)}) collective-permute-start(f32[1,1,256,512]{3,2,1,0:T(8,128)S(1)} %get-tuple-element.42), channel_id=1, source_target_pairs={{0,1},{1,2},{2,3},{3,4},{4,5},{5,6},{6,7},{7,8},{8,9},{9,10},{10,1... | collective-permute-start | bytes 1572872 | tf_op jit(solution)/shard_map/ppermute | solution.py:26
  204.9 16.7 %copy-start.1 = (f32[4,256,512]{2,1,0:T(8,128)S(1)}, f32[4,256,512]{2,1,0:T(8,128)}, u32[]{:S(2)}) copy-start(f32[4,256,512]{2,1,0:T(8,128)} %param.3) | copy-start | bytes 6291460
  205.0 14.4 %collective-permute-start.14 = (f32[1,1,256,512]{3,2,1,0:T(8,128)S(1)}, f32[1,1,256,512]{3,2,1,0:T(8,128)S(1)}, u32[]{:S(2)}, u32[]{:S(2)}) collective-permute-start(f32[1,1,256,512]{3,2,1,0:T(8,128)S(1)} %get-tuple-element.43), channel_id=1, source_target_pairs={{1,0},{2,1},{3,2},{4,3},{5,4},{6,5},{7,6},{8,7},{9,8},{10,9},{11,1... | collective-permute-start | bytes 1572872 | tf_op jit(solution)/shard_map/ppermute | solution.py:29
  258.9 4.5 collective-permute-start.17
  265.5 79.8 %copy-start.10 = (f32[1,4,256,512]{3,2,1,0:T(8,128)}, f32[1,4,256,512]{3,2,1,0:T(8,128)S(1)}, u32[]{:S(2)}) copy-start(f32[1,4,256,512]{3,2,1,0:T(8,128)S(1)} %dynamic-slice_select_fusion.1) | copy-start | bytes 6291460
  265.5 19.1 %copy-start.6 = (f32[1,4,256,512]{3,2,1,0:T(8,128)S(1)}, f32[1,4,256,512]{3,2,1,0:T(8,128)}, u32[]{:S(2)}) copy-start(f32[1,4,256,512]{3,2,1,0:T(8,128)} %copy-done.4) | copy-start | bytes 6291460
  265.6 14.8 %collective-permute-start.18 = (f32[1,1,256,512]{3,2,1,0:T(8,128)S(1)}, f32[1,1,256,512]{3,2,1,0:T(8,128)S(1)}, u32[]{:S(2)}, u32[]{:S(2)}) collective-permute-start(f32[1,1,256,512]{3,2,1,0:T(8,128)S(1)} %get-tuple-element.40), channel_id=1, source_target_pairs={{0,1},{1,2},{2,3},{3,4},{4,5},{5,6},{6,7},{7,8},{8,9},{9,10},{10,1... | collective-permute-start | bytes 1572872 | tf_op jit(solution)/shard_map/ppermute | solution.py:26
  268.4 16.2 %collective-permute-start.19 = (f32[1,1,256,512]{3,2,1,0:T(8,128)S(1)}, f32[1,1,256,512]{3,2,1,0:T(8,128)S(1)}, u32[]{:S(2)}, u32[]{:S(2)}) collective-permute-start(f32[1,1,256,512]{3,2,1,0:T(8,128)S(1)} %get-tuple-element.41), channel_id=1, source_target_pairs={{1,0},{2,1},{3,2},{4,3},{5,4},{6,5},{7,6},{8,7},{9,8},{10,9},{11,1... | collective-permute-start | bytes 1572872 | tf_op jit(solution)/shard_map/ppermute | solution.py:29
  304.2 18.4 %copy-start.17 = (f32[1,6,256,512]{3,2,1,0:T(8,128)}, f32[1,6,256,512]{3,2,1,0:T(8,128)S(1)}, u32[]{:S(2)}) copy-start(f32[1,6,256,512]{3,2,1,0:T(8,128)S(1)} %fusion.209) | copy-start | bytes 9437188
  304.2 13.4 %collective-permute-start.20 = (f32[1,1,256,512]{3,2,1,0:T(8,128)S(1)}, f32[1,1,256,512]{3,2,1,0:T(8,128)S(1)}, u32[]{:S(2)}, u32[]{:S(2)}) collective-permute-start(f32[1,1,256,512]{3,2,1,0:T(8,128)S(1)} %get-tuple-element.28), channel_id=1, source_target_pairs={{0,1},{1,2},{2,3},{3,4},{4,5},{5,6},{6,7},{7,8},{8,9},{9,10},{10,1... | collective-permute-start | bytes 1572872 | tf_op jit(solution)/shard_map/ppermute | solution.py:26
  306.7 15.5 %collective-permute-start.21 = (f32[1,1,256,512]{3,2,1,0:T(8,128)S(1)}, f32[1,1,256,512]{3,2,1,0:T(8,128)S(1)}, u32[]{:S(2)}, u32[]{:S(2)}) collective-permute-start(f32[1,1,256,512]{3,2,1,0:T(8,128)S(1)} %get-tuple-element.29), channel_id=1, source_target_pairs={{1,0},{2,1},{3,2},{4,3},{5,4},{6,5},{7,6},{8,7},{9,8},{10,9},{11,1... | collective-permute-start | bytes 1572872 | tf_op jit(solution)/shard_map/ppermute | solution.py:29
  323.1 15.7 %collective-permute-start.23 = (f32[1,1,256,512]{3,2,1,0:T(8,128)S(1)}, f32[1,1,256,512]{3,2,1,0:T(8,128)S(1)}, u32[]{:S(2)}, u32[]{:S(2)}) collective-permute-start(f32[1,1,256,512]{3,2,1,0:T(8,128)S(1)} %get-tuple-element.38), channel_id=1, source_target_pairs={{0,1},{1,2},{2,3},{3,4},{4,5},{5,6},{6,7},{7,8},{8,9},{9,10},{10,1... | collective-permute-start | bytes 1572872 | tf_op jit(solution)/shard_map/ppermute | solution.py:26
  328.7 16.7 %copy-start.2 = (f32[4,256,512]{2,1,0:T(8,128)S(1)}, f32[4,256,512]{2,1,0:T(8,128)}, u32[]{:S(2)}) copy-start(f32[4,256,512]{2,1,0:T(8,128)} %param.3) | copy-start | bytes 6291460
  328.7 14.4 %collective-permute-start.22 = (f32[1,1,256,512]{3,2,1,0:T(8,128)S(1)}, f32[1,1,256,512]{3,2,1,0:T(8,128)S(1)}, u32[]{:S(2)}, u32[]{:S(2)}) collective-permute-start(f32[1,1,256,512]{3,2,1,0:T(8,128)S(1)} %get-tuple-element.39), channel_id=1, source_target_pairs={{1,0},{2,1},{3,2},{4,3},{5,4},{6,5},{7,6},{8,7},{9,8},{10,9},{11,1... | collective-permute-start | bytes 1572872 | tf_op jit(solution)/shard_map/ppermute | solution.py:29
  383.3 4.5 collective-permute-start.25
  385.0 9.4 %collective-permute-start.8 = (f32[1,4,256,512]{3,2,1,0:T(8,128)}, f32[1,4,256,512]{3,2,1,0:T(8,128)}, u32[]{:S(2)}, u32[]{:S(2)}) collective-permute-start(f32[1,4,256,512]{3,2,1,0:T(8,128)} %broadcast_multiply_fusion), channel_id=1, source_target_pairs={{0,64},{64,0},{1,65},{65,1},{2,66},{66,2},{3,67},{67,3},{4,68},{68... | collective-permute-start | bytes 6291464 | tf_op jit(solution)/shard_map/ppermute | solution.py:55
  390.0 79.6 %copy-start.8 = (f32[1,4,256,512]{3,2,1,0:T(8,128)}, f32[1,4,256,512]{3,2,1,0:T(8,128)S(1)}, u32[]{:S(2)}) copy-start(f32[1,4,256,512]{3,2,1,0:T(8,128)S(1)} %dynamic-slice_select_fusion) | copy-start | bytes 6291460
  390.2 14.8 %collective-permute-start.26 = (f32[1,1,256,512]{3,2,1,0:T(8,128)S(1)}, f32[1,1,256,512]{3,2,1,0:T(8,128)S(1)}, u32[]{:S(2)}, u32[]{:S(2)}) collective-permute-start(f32[1,1,256,512]{3,2,1,0:T(8,128)S(1)} %get-tuple-element.36), channel_id=1, source_target_pairs={{0,1},{1,2},{2,3},{3,4},{4,5},{5,6},{6,7},{7,8},{8,9},{9,10},{10,1... | collective-permute-start | bytes 1572872 | tf_op jit(solution)/shard_map/ppermute | solution.py:26
  392.9 16.3 %collective-permute-start.27 = (f32[1,1,256,512]{3,2,1,0:T(8,128)S(1)}, f32[1,1,256,512]{3,2,1,0:T(8,128)S(1)}, u32[]{:S(2)}, u32[]{:S(2)}) collective-permute-start(f32[1,1,256,512]{3,2,1,0:T(8,128)S(1)} %get-tuple-element.37), channel_id=1, source_target_pairs={{1,0},{2,1},{3,2},{4,3},{5,4},{6,5},{7,6},{8,7},{9,8},{10,9},{11,1... | collective-permute-start | bytes 1572872 | tf_op jit(solution)/shard_map/ppermute | solution.py:29
  395.1 59.4 %collective-permute-start.16 = (f32[1,4,256,512]{3,2,1,0:T(8,128)S(1)}, f32[1,4,256,512]{3,2,1,0:T(8,128)S(1)}, u32[]{:S(2)}, u32[]{:S(2)}) collective-permute-start(f32[1,4,256,512]{3,2,1,0:T(8,128)S(1)} %multiply_add_fusion.2), channel_id=1, source_target_pairs={{0,64},{64,0},{1,65},{65,1},{2,66},{66,2},{3,67},{67,3},{4,68},{68... | collective-permute-start | bytes 6291464 | tf_op jit(solution)/shard_map/ppermute | solution.py:55
  428.9 18.3 %copy-start.13 = (f32[1,6,256,512]{3,2,1,0:T(8,128)}, f32[1,6,256,512]{3,2,1,0:T(8,128)S(1)}, u32[]{:S(2)}) copy-start(f32[1,6,256,512]{3,2,1,0:T(8,128)S(1)} %fusion.273) | copy-start | bytes 9437188
  429.0 13.4 %collective-permute-start.28 = (f32[1,1,256,512]{3,2,1,0:T(8,128)S(1)}, f32[1,1,256,512]{3,2,1,0:T(8,128)S(1)}, u32[]{:S(2)}, u32[]{:S(2)}) collective-permute-start(f32[1,1,256,512]{3,2,1,0:T(8,128)S(1)} %get-tuple-element.26), channel_id=1, source_target_pairs={{0,1},{1,2},{2,3},{3,4},{4,5},{5,6},{6,7},{7,8},{8,9},{9,10},{10,1... | collective-permute-start | bytes 1572872 | tf_op jit(solution)/shard_map/ppermute | solution.py:26
  431.4 15.5 %collective-permute-start.29 = (f32[1,1,256,512]{3,2,1,0:T(8,128)S(1)}, f32[1,1,256,512]{3,2,1,0:T(8,128)S(1)}, u32[]{:S(2)}, u32[]{:S(2)}) collective-permute-start(f32[1,1,256,512]{3,2,1,0:T(8,128)S(1)} %get-tuple-element.27), channel_id=1, source_target_pairs={{1,0},{2,1},{3,2},{4,3},{5,4},{6,5},{7,6},{8,7},{9,8},{10,9},{11,1... | collective-permute-start | bytes 1572872 | tf_op jit(solution)/shard_map/ppermute | solution.py:29
  447.3 15.9 %collective-permute-start.31 = (f32[1,1,256,512]{3,2,1,0:T(8,128)S(1)}, f32[1,1,256,512]{3,2,1,0:T(8,128)S(1)}, u32[]{:S(2)}, u32[]{:S(2)}) collective-permute-start(f32[1,1,256,512]{3,2,1,0:T(8,128)S(1)} %get-tuple-element.34), channel_id=1, source_target_pairs={{0,1},{1,2},{2,3},{3,4},{4,5},{5,6},{6,7},{7,8},{8,9},{9,10},{10,1... | collective-permute-start | bytes 1572872 | tf_op jit(solution)/shard_map/ppermute | solution.py:26
  453.1 14.2 %collective-permute-start.30 = (f32[1,1,256,512]{3,2,1,0:T(8,128)S(1)}, f32[1,1,256,512]{3,2,1,0:T(8,128)S(1)}, u32[]{:S(2)}, u32[]{:S(2)}) collective-permute-start(f32[1,1,256,512]{3,2,1,0:T(8,128)S(1)} %get-tuple-element.35), channel_id=1, source_target_pairs={{1,0},{2,1},{3,2},{4,3},{5,4},{6,5},{7,6},{8,7},{9,8},{10,9},{11,1... | collective-permute-start | bytes 1572872 | tf_op jit(solution)/shard_map/ppermute | solution.py:29
  456.5 49.9 %collective-permute-start.24 = (f32[1,4,256,512]{3,2,1,0:T(8,128)}, f32[1,4,256,512]{3,2,1,0:T(8,128)}, u32[]{:S(2)}, u32[]{:S(2)}) collective-permute-start(f32[1,4,256,512]{3,2,1,0:T(8,128)} %multiply_add_fusion.1), channel_id=1, source_target_pairs={{0,64},{64,0},{1,65},{65,1},{2,66},{66,2},{3,67},{67,3},{4,68},{68... | collective-permute-start | bytes 6291464 | tf_op jit(solution)/shard_map/ppermute | solution.py:55
  506.3 7.6 %collective-permute-start.33 = (f32[1,4,256,512]{3,2,1,0:T(8,128)S(1)}, f32[1,4,256,512]{3,2,1,0:T(8,128)}, u32[]{:S(2)}, u32[]{:S(2)}) collective-permute-start(f32[1,4,256,512]{3,2,1,0:T(8,128)S(1)} %multiply_subtract_fusion), channel_id=1, source_target_pairs={{0,64},{64,0},{1,65},{65,1},{2,66},{66,2},{3,67},{67,3},{4,68},{68... | collective-permute-start | bytes 6291464 | tf_op jit(solution)/shard_map/ppermute | solution.py:55
  508.6 41.5 %collective-permute-start.32 = (f32[1,4,256,512]{3,2,1,0:T(8,128)}, f32[1,4,256,512]{3,2,1,0:T(8,128)}, u32[]{:S(2)}, u32[]{:S(2)}) collective-permute-start(f32[1,4,256,512]{3,2,1,0:T(8,128)} %multiply_add_fusion), channel_id=1, source_target_pairs={{0,64},{64,0},{1,65},{65,1},{2,66},{66,2},{3,67},{67,3},{4,68},{68... | collective-permute-start | bytes 6291464 | tf_op jit(solution)/shard_map/ppermute | solution.py:55
  (19 other events, 137.5 us)
where the time goes:
time: 564 us; the launch traced here: 554 us
  waiting for transfers between devices  169 us (30%)
  other arithmetic  156 us (28%)
  blocking collectives  139 us (25%)
  starting transfers between devices  73.2 us (13%)
  local copies, waits for them, and re-layouts  9.26 us (2%)
  between operations  7.25 us (1%)
    all_to_all x4, blocking collectives, from_everyone(): return lax.all_to_all(copies, axis, split_axis=0, concat_axis=0, tiled=True)  110 us
    ppermute x13, waiting for transfers between devices, extended_2(): lax.ppermute(lax.slice_in_dim(block, block.shape[dim] - width, None, axis...  101 us
    mul x28, other arithmetic, jacobi(): found = (found + scale * (resid - (6.0 + diag) * found + beside)) * mask  69.5 us
    ppermute x13, waiting for transfers between devices, extended_2(): lax.ppermute(lax.slice_in_dim(block, 0, width, axis=dim), axis, backward)  56.7 us
    ppermute x13, starting transfers between devices, extended_2(): lax.ppermute(lax.slice_in_dim(block, block.shape[dim] - width, None, axis...  49.5 us
    psum x4, blocking collectives, by_axis(): shard = lax.psum(shard, axis)  29.1 us
    ppermute x13, starting transfers between devices, extended_2(): lax.ppermute(lax.slice_in_dim(block, 0, width, axis=dim), axis, backward)  18.4 us
    sub x4, other arithmetic, colour_step(): return (current + alpha * correction, resid - alpha * image)  16.1 us
  transfers between devices with their start and end apart: 34, of which 28 were waited for; matrix products, arithmetic and copies ran while one was open for 10% of the time, Pallas kernels for 0%

commit v1 on v0

v1 whole, which is shorter than its diff:
```python
import functools

import jax
import jax.numpy as jnp
from jax import lax
from jax.experimental import pallas as pl
from jax.experimental.pallas import tpu as pltpu
from jax.sharding import Mesh
from jax.sharding import PartitionSpec as P

OMEGA = 0.8
SWEEPS = 8
NY = 256
NZ = 512
NRHS = 3
OWN = 128
WIN = 144
K = WIN // 8
LANES = 128
TILES = NZ // LANES
SUB = ("sub_0", "sub_1", "sub_2")
VMEM_LIMIT = 32 * 1024 * 1024


def powers():
    total = [0.0] * SWEEPS
    power = [1.0]
    for _ in range(SWEEPS):
        for i, value in enumerate(power):
            total[i] += value
        longer = [0.0] * (len(power) + 1)
        for i, value in enumerate(power):
            longer[i] += (1.0 - OMEGA) * value
            longer[i + 1] += value
        power = longer
    return total


COEFFICIENTS = powers()
PLANE = (K, 8, NZ)


def shape_of(*lead):
    return jax.ShapeDtypeStruct((*lead, *PLANE), jnp.float32)


def tile(t):
    return slice(t * LANES, (t + 1) * LANES)


def lanes():
    return lax.broadcasted_iota(jnp.int32, (8, LANES), 1)


def sublanes():
    return lax.broadcasted_iota(jnp.int32, (8, LANES), 0)


def owned(k, colour):
    row = sublanes() * K + k - colour * (WIN - OWN)
    return (row >= 0) & (row < OWN)


def close_edges(buf):
    sub = sublanes()
    for p in range(4):
        for t in range(TILES):
            last = pltpu.roll(buf[p, K, :, tile(t)], 1, 0)
            buf[p, 0, :, tile(t)] = jnp.where(sub == 0, 0.0, last)
            first = pltpu.roll(buf[p, 1, :, tile(t)], 7, 0)
            buf[p, K + 1, :, tile(t)] = jnp.where(sub == 7, 0.0, first)


def beside(buf, k):
    lane = lanes()
    first, last = lane == 0, lane == LANES - 1
    here = [[buf[p, k + 1, :, tile(t)] for t in range(TILES)] for p in range(4)]
    sums = []
    for p in range(4):
        up = [pltpu.roll(v, 1, 1) for v in here[p]]
        down = [pltpu.roll(v, LANES - 1, 1) for v in here[p]]
        row = []
        for t in range(TILES):
            total = jnp.where(first, up[t - 1] if t else 0.0, up[t])
            total = total + jnp.where(last, down[t + 1] if t + 1 < TILES else 0.0, down[t])
            total = total + (buf[p, k, :, tile(t)] + buf[p, k + 2, :, tile(t)])
            if p == 0:
                total = total + here[1][t]
            elif p == 3:
                total = total + here[2][t]
            else:
                total = total + (here[p - 1][t] + here[p + 1][t])
            row.append(total)
        sums.append(row)
    return sums, here


def solve(source, scale, one, two):
    close_edges(one)
    bufs = (one, two)
    for step, power in enumerate(range(SWEEPS - 2, -1, -1)):
        src, dst = bufs[step % 2], bufs[1 - step % 2]
        factor = COEFFICIENTS[power]

        def body(k, _, src=src, dst=dst, factor=factor):
            sums, _ = beside(src, k)
            for p in range(4):
                for t in range(TILES):
                    dst[p, k + 1, :, tile(t)] = (
                        scale[p, k, :, tile(t)] * sums[p][t]
                        + factor * source[p, k, :, tile(t)]
                    )
            return 0

        lax.fori_loop(0, K, body, 0)
        close_edges(dst)
    return bufs[(SWEEPS - 1) % 2]


def prepare_kernel(planes, at, *refs):
    where, rhs, diag = at, refs[0], refs[1]
    count = NRHS + 1
    outs = refs[2 : 2 + len(planes) * count]
    held, sem = refs[2 + len(planes) * count :]
    low = pl.multiple_of(where[0] * (NY - WIN), 8)
    copies = []
    for i, plane in enumerate(planes):
        for r in range(count):
            for t in range(TILES):
                if r < NRHS:
                    src = rhs.at[r, plane, pl.ds(low, WIN), tile(t)]
                else:
                    src = diag.at[plane, pl.ds(low, WIN), tile(t)]
                copies.append(
                    pltpu.make_async_copy(src, held.at[i * count + r, t], sem.at[i * count + r, t])
                )
    for copy in copies:
        copy.start()
    for n, out in enumerate(outs):
        for t in range(TILES):
            copies[n * TILES + t].wait()
            for k in range(K):
                out[k, :, tile(t)] = held[n, t, pl.ds(k, 8, stride=K), :]


def prepare(planes, where, rhs, diag):
    count = len(planes) * (NRHS + 1)
    return pl.pallas_call(
        functools.partial(prepare_kernel, planes),
        out_shape=[shape_of()] * count,
        in_specs=[
            pl.BlockSpec(memory_space=pltpu.SMEM),
            pl.BlockSpec(memory_space=pl.ANY),
            pl.BlockSpec(memory_space=pl.ANY),
        ],
        out_specs=[pl.BlockSpec(memory_space=pltpu.VMEM)] * count,
        scratch_shapes=[
            pltpu.VMEM((count, TILES, WIN, LANES), jnp.float32),
            pltpu.SemaphoreType.DMA((count, TILES)),
        ],
        compiler_params=pltpu.CompilerParams(vmem_limit_bytes=VMEM_LIMIT),
        cost_estimate=pl.CostEstimate(flops=0, bytes_accessed=count * 600000, transcendentals=0),
    )(where, rhs, diag)


def local(buf, diags, k):
    sums, here = beside(buf, k)
    images = [
        [(6.0 + diags[p][k, :, tile(t)]) * here[p][t] - sums[p][t] for t in range(TILES)]
        for p in range(4)
    ]
    return images, here


def fill(k, p, q, d, keep, scale, source, one):
    for t in range(TILES):
        s = OMEGA / (6.0 + d[k, :, tile(t)])
        if keep is not None:
            s = s * keep
        g = s * q[t]
        scale[p, k, :, tile(t)] = s
        source[p, k, :, tile(t)] = g
        one[p, k + 1, :, tile(t)] = g


SCRATCH = [
    pltpu.VMEM((4, K, 8, NZ), jnp.float32),
    pltpu.VMEM((4, K, 8, NZ), jnp.float32),
    pltpu.VMEM((4, K + 2, 8, NZ), jnp.float32),
    pltpu.VMEM((4, K + 2, 8, NZ), jnp.float32),
]


def first_kernel(where, qh, q0, q1, q2, dh, d0, d1, d2, ch, c, t2, t12, sums, scale, source, one, two):
    colour, device = where[0], where[1]
    keep = (device > 0).astype(jnp.float32)
    qs, ds = (qh, q0, q1, q2), (dh, d0, d1, d2)

    def start(k, _):
        for p in range(4):
            q = [qs[p][k, :, tile(t)] for t in range(TILES)]
            fill(k, p, q, ds[p], keep if p == 0 else None, scale, source, one)
        return 0

    lax.fori_loop(0, K, start, 0)
    found = solve(source, scale, one, two)

    def finish(k, carry):
        upper, lower = carry
        images, here = local(found, ds, k)
        mask = owned(k, colour)
        up, low = 0.0, 0.0
        for p in range(4):
            for t in range(TILES):
                value = here[p][t]
                up = up + qs[p][k, :, tile(t)] * value
                low = low + images[p][t] * value
                if p == 0:
                    ch[k, :, tile(t)] = value
                else:
                    c[p - 1, k, :, tile(t)] = value
                if p < 2:
                    t2[p, k, :, tile(t)] = images[p][t]
                else:
                    t12[p - 2, k, :, tile(t)] = images[p][t]
        return upper + jnp.where(mask, up, 0.0), lower + jnp.where(mask, low, 0.0)

    zero = jnp.zeros((8, LANES), jnp.float32)
    upper, lower = lax.fori_loop(0, K, finish, (zero, zero))
    sums[0] = upper
    sums[1] = lower


VM = pl.BlockSpec(memory_space=pltpu.VMEM)
SM = pl.BlockSpec(memory_space=pltpu.SMEM)


def estimate(planes, passes):
    return pl.CostEstimate(
        flops=passes * 4 * K * 8 * NZ * 10, bytes_accessed=planes * K * 8 * NZ * 4, transcendentals=0
    )


def first_solve(where, *arrays):
    return pl.pallas_call(
        first_kernel,
        out_shape=[
            shape_of(),
            shape_of(3),
            shape_of(2),
            shape_of(2),
            jax.ShapeDtypeStruct((2, 8, LANES), jnp.float32),
        ],
        in_specs=[SM] + [VM] * 8,
        out_specs=[VM] * 5,
        scratch_shapes=SCRATCH,
        compiler_params=pltpu.CompilerParams(vmem_limit_bytes=VMEM_LIMIT),
        cost_estimate=estimate(16, SWEEPS + 1),
    )(where, *arrays)


def rows_of(values, count):
    rows = [jnp.sum(v, axis=0, keepdims=True) for v in values]
    rows += [jnp.zeros((1, LANES), jnp.float32)] * (count - len(rows))
    return jnp.concatenate(rows, axis=0)


def join_kernel(where, *refs):
    cs, rights, sums, out = refs[:NRHS], refs[NRHS : 2 * NRHS], refs[2 * NRHS : 3 * NRHS], refs[-1]
    colour = where[0]
    zero = jnp.zeros((8, LANES), jnp.float32)
    uppers, lowers = [], []
    for r in range(NRHS):

        def body(k, total, r=r):
            add = 0.0
            for t in range(TILES):
                add = add + cs[r][2, k, :, tile(t)] * rights[r][k, :, tile(t)]
            return total + jnp.where(owned(k, colour), add, 0.0)

        between = lax.fori_loop(0, K, body, zero)
        uppers.append(sums[r][0])
        lowers.append(sums[r][1] - 2.0 * between)
    out[...] = rows_of(uppers + lowers, 8)


def join(where, cs, rights, sums):
    return pl.pallas_call(
        join_kernel,
        out_shape=jax.ShapeDtypeStruct((8, LANES), jnp.float32),
        in_specs=[SM] + [VM] * (3 * NRHS),
        out_specs=VM,
        compiler_params=pltpu.CompilerParams(vmem_limit_bytes=VMEM_LIMIT),
        cost_estimate=estimate(12, 1),
    )(where, *cs, *rights, *sums)


def ratio(table, upper, lower):
    top = jnp.sum(table[upper : upper + 1, :], axis=1, keepdims=True)
    bottom = jnp.sum(table[lower : lower + 1, :], axis=1, keepdims=True)
    return top / bottom


def second_kernel(
    r, where, table, q1, q2, q3, q4, d1, d2, d3, d4, c, cr, tr, t12,
    ca, cm, cd, ta, tm, td, res, sums, scale, source, one, two,
):
    colour, device, count = where[0], where[1], where[2]
    keep = (device < count - 1).astype(jnp.float32)
    alpha = jnp.broadcast_to(ratio(table, r, NRHS + r), (8, LANES))
    ds = (d1, d2, d3, d4)

    def start(k, _):
        for p in range(4):
            values = []
            for t in range(TILES):
                if p == 0:
                    image = t12[0, k, :, tile(t)]
                    q = q1[k, :, tile(t)]
                elif p == 1:
                    image = t12[1, k, :, tile(t)] - cr[k, :, tile(t)]
                    q = q2[k, :, tile(t)]
                elif p == 2:
                    image = tr[0, k, :, tile(t)] - c[2, k, :, tile(t)]
                    q = q3[k, :, tile(t)]
                else:
                    image = tr[1, k, :, tile(t)]
                    q = q4[k, :, tile(t)]
                value = q - alpha * image
                res[p, k, :, tile(t)] = value
                values.append(value)
            fill(k, p, values, ds[p], keep if p == 3 else None, scale, source, one)
        return 0

    lax.fori_loop(0, K, start, 0)
    found = solve(source, scale, one, two)

    def finish(k, carry):
        images, here = local(found, ds, k)
        mask = owned(k, colour)
        adds = [0.0] * 5
        for p in range(4):
            for t in range(TILES):
                value, image, q = here[p][t], images[p][t], res[p, k, :, tile(t)]
                adds[0] = adds[0] + q * value
                adds[1] = adds[1] + image * value
                if p in (1, 2):
                    rest = q - image
                    adds[2] = adds[2] + rest * rest
                    adds[3] = adds[3] + rest * image
                    adds[4] = adds[4] + image * image
                    cm[p - 1, k, :, tile(t)] = value
                    tm[p - 1, k, :, tile(t)] = image
                else:
                    (ca if p == 0 else cd)[k, :, tile(t)] = value
                    (ta if p == 0 else td)[k, :, tile(t)] = image
        return tuple(a + jnp.where(mask, b, 0.0) for a, b in zip(carry, adds))

    zero = jnp.zeros((8, LANES), jnp.float32)
    found_sums = lax.fori_loop(0, K, finish, (zero,) * 5)
    for i in range(5):
        sums[i] = found_sums[i]


def second_solve(r, where, table, *arrays):
    return pl.pallas_call(
        functools.partial(second_kernel, r),
        out_shape=[
            shape_of(),
            shape_of(2),
            shape_of(),
            shape_of(),
            shape_of(2),
            shape_of(),
            shape_of(4),
            jax.ShapeDtypeStruct((5, 8, LANES), jnp.float32),
        ],
        in_specs=[SM] + [VM] * 13,
        out_specs=[VM] * 8,
        scratch_shapes=SCRATCH,
        compiler_params=pltpu.CompilerParams(vmem_limit_bytes=VMEM_LIMIT),
        cost_estimate=estimate(28, SWEEPS + 1),
    )(where, table, *arrays)


def join_second_kernel(where, table, *refs):
    out = refs[-1]
    colour, device, count = where[0], where[1], where[2]
    begin = (device == 0).astype(jnp.float32)
    inside = (device < count - 1).astype(jnp.float32)
    zero = jnp.zeros((8, LANES), jnp.float32)
    rows = [[] for _ in range(5)]
    for r in range(NRHS):
        res, ca, cd, ta, td, cl, cr, q0, t2, sums = refs[10 * r : 10 * r + 10]
        alpha = jnp.broadcast_to(ratio(table, r, NRHS + r), (8, LANES))

        def body(k, carry, res=res, ca=ca, cd=cd, ta=ta, td=td, cl=cl, cr=cr, q0=q0, t2=t2, alpha=alpha):
            between = 0.0
            parts = [[0.0] * 3 for _ in range(3)]
            for t in range(TILES):
                at = (k, slice(None), tile(t))
                between = between + ca[at] * cl[at] + cd[at] * cr[at]
                for n, (q, image) in enumerate(
                    (
                        (res[(0, *at)], ta[at] - cl[at]),
                        (res[(3, *at)], td[at] - cr[at]),
                        (q0[at] - alpha * t2[(1, *at)], -ca[at]),
                    )
                ):
                    rest = q - image
                    parts[n][0] = parts[n][0] + rest * rest
                    parts[n][1] = parts[n][1] + rest * image
                    parts[n][2] = parts[n][2] + image * image
            adds = [between] + [a + inside * b + begin * c for a, b, c in zip(*parts)]
            mask = owned(k, colour)
            return tuple(a + jnp.where(mask, b, 0.0) for a, b in zip(carry, adds))

        between, *squares = lax.fori_loop(0, K, body, (zero,) * 4)
        rows[0].append(sums[0])
        rows[1].append(sums[1] - between)
        for i in range(3):
            rows[2 + i].append(sums[2 + i] + squares[i])
    out[...] = rows_of([value for row in rows for value in row], 16)


def join_second(where, table, arrays):
    return pl.pallas_call(
        join_second_kernel,
        out_shape=jax.ShapeDtypeStruct((16, LANES), jnp.float32),
        in_specs=[SM] + [VM] * (1 + 10 * NRHS),
        out_specs=VM,
        compiler_params=pltpu.CompilerParams(vmem_limit_bytes=VMEM_LIMIT),
        cost_estimate=estimate(40, 2),
    )(where, table, *arrays)


def last_kernel(where, table, after, *refs):
    norms, mine_u, mine_q, held, sems = refs[-5:]
    colour = where[0]
    low = pl.multiple_of(colour * (WIN - OWN), 8)
    rows = []
    pending = []
    for r in range(NRHS):
        q0, t2, c, c3, res, c0l, ca, cm, t0l, ta, tm = refs[11 * r : 11 * r + 11]
        first = ratio(table, r, NRHS + r)
        second = ratio(after, r, NRHS + r)
        more = second - 1.0
        square, cross, own = (
            jnp.sum(after[i * NRHS + r : i * NRHS + r + 1, :], axis=1, keepdims=True) for i in (2, 3, 4)
        )
        total = square - 2.0 * more * cross + more * more * own
        rows.append(jnp.broadcast_to(jnp.sqrt(jnp.maximum(total, 0.0)), (1, LANES)))
        one = jnp.broadcast_to(first, (8, LANES))
        two = jnp.broadcast_to(second, (8, LANES))
        slot = r % 2
        if r >= 2:
            for copy in pending[r - 2]:
                copy.wait()

        def body(k, _, q0=q0, t2=t2, c=c, c3=c3, res=res, c0l=c0l, ca=ca, cm=cm, t0l=t0l, ta=ta, tm=tm, one=one, two=two, slot=slot):
            for t in range(TILES):
                at = (k, slice(None), tile(t))
                firsts = [c[(0, *at)], c[(1, *at)], c[(2, *at)], c3[at]]
                seconds = [c0l[at], ca[at], cm[(0, *at)], cm[(1, *at)]]
                residuals = [q0[at] - one * t2[(1, *at)], res[(0, *at)], res[(1, *at)], res[(2, *at)]]
                images = [t0l[at] - ca[at], ta[at] - c0l[at], tm[(0, *at)], tm[(1, *at)]]
                for p in range(4):
                    rows_at = pl.ds(k, 8, stride=K)
                    held[slot, 0, p, t, rows_at, :] = one * firsts[p] + two * seconds[p]
                    held[slot, 1, p, t, rows_at, :] = residuals[p] - two * images[p]
            return 0

        lax.fori_loop(0, K, body, 0)
        copies = []
        for n, out in enumerate((mine_u, mine_q)):
            for t in range(TILES):
                copies.append(
                    pltpu.make_async_copy(
                        held.at[slot, n, :, t, pl.ds(low, OWN), :],
                        out.at[t // (TILES // 2), r, :, :, tile(t % (TILES // 2))],
                        sems.at[slot, n, t],
                    )
                )
        for copy in copies:
            copy.start()
        pending.append(copies)
    for copies in pending[max(0, NRHS - 2) :]:
        for copy in copies:
            copy.wait()
    rows += [jnp.zeros((1, LANES), jnp.float32)] * (8 - NRHS)
    norms[...] = jnp.concatenate(rows, axis=0)


def last(where, table, after, arrays):
    halves = jax.ShapeDtypeStruct((2, NRHS, 4, OWN, NZ // 2), jnp.float32)
    return pl.pallas_call(
        last_kernel,
        out_shape=[jax.ShapeDtypeStruct((8, LANES), jnp.float32), halves, halves],
        in_specs=[SM] + [VM] * (2 + 11 * NRHS),
        out_specs=[VM, pl.BlockSpec(memory_space=pl.ANY), pl.BlockSpec(memory_space=pl.ANY)],
        scratch_shapes=[
            pltpu.VMEM((2, 2, 4, TILES, WIN, LANES), jnp.float32),
            pltpu.SemaphoreType.DMA((2, 2, TILES)),
        ],
        compiler_params=pltpu.CompilerParams(vmem_limit_bytes=40 * 1024 * 1024),
        cost_estimate=estimate(70, 3),
    )(where, table, after, *arrays)


def everywhere(value):
    value = value + lax.ppermute(value, "colour", [(0, 1), (1, 0)])
    for axis in reversed(SUB):
        count = lax.axis_size(axis)
        a, b, c = (
            lax.ppermute(value, axis, [(i, i ^ mask) for i in range(count)]) for mask in (1, 2, 3)
        )
        value = (value + a) + (b + c)
    return value


def shards(rhs, diagonal):
    colour = lax.axis_index("colour")
    device = lax.axis_index(SUB)
    total = lax.axis_size(SUB)
    forward = [(i, i + 1) for i in range(total - 1)]
    backward = [(i + 1, i) for i in range(total - 1)]
    where = jnp.stack([colour, device, jnp.int32(total)]).astype(jnp.int32)

    def right(value):
        return lax.ppermute(value, SUB, forward)

    def left(value):
        return lax.ppermute(value, SUB, backward)

    *q0, d0 = (outer := prepare((0, 3), where, rhs, diagonal))[: NRHS + 1]
    *q3, d3 = outer[NRHS + 1 :]
    dh = right(d3)
    qh = [right(q) for q in q3]
    d4 = left(d0)
    q4 = [left(q) for q in q0]
    *q1, d1 = (inner := prepare((1, 2), where, rhs, diagonal))[: NRHS + 1]
    *q2, d2 = inner[NRHS + 1 :]

    firsts = [
        first_solve(where, qh[r], q0[r], q1[r], q2[r], dh, d0, d1, d2) for r in range(NRHS)
    ]
    ch, c, t2, t12, sums = zip(*firsts)
    cr = [left(v) for v in ch]
    tr = [left(v) for v in t2]
    table = everywhere(join(where, c, cr, sums))
    seconds = [
        second_solve(
            r, where, table, q1[r], q2[r], q3[r], q4[r], d1, d2, d3, d4, c[r], cr[r], tr[r], t12[r]
        )
        for r in range(NRHS)
    ]
    ca, cm, cd, ta, tm, td, res, sums = zip(*seconds)
    cl = [right(v) for v in cd]
    cr1 = [left(v) for v in ca]
    tl = [right(v) for v in td]
    arrays = [
        a
        for r in range(NRHS)
        for a in (res[r], ca[r], cd[r], ta[r], td[r], cl[r], cr1[r], q0[r], t2[r], sums[r])
    ]
    after = everywhere(join_second(where, table, arrays))
    arrays = [
        a
        for r in range(NRHS)
        for a in (q0[r], t2[r], c[r], cr[r], res[r], cl[r], ca[r], cm[r], tl[r], ta[r], tm[r])
    ]
    norms, us, qs = last(where, table, after, arrays)

    def whole(halves):
        mine = lax.dynamic_index_in_dim(halves, colour, 0, keepdims=False)
        other = lax.dynamic_index_in_dim(halves, 1 - colour, 0, keepdims=False)
        other = lax.ppermute(other, "colour", [(0, 1), (1, 0)])
        first = jnp.where(colour == 0, mine, other)
        second = jnp.where(colour == 0, other, mine)
        return jnp.concatenate([first, second], axis=2)

    return whole(us), whole(qs), norms[:NRHS, 0]


def solution(mesh):
    torus = Mesh(
        mesh.devices.reshape(mesh.shape["colour"], 4, 4, 4), ("colour", "sub_0", "sub_1", "sub_2")
    )
    return jax.shard_map(
        shards,
        mesh=torus,
        in_specs=(P(None, SUB, None, None), P(SUB, None, None)),
        out_specs=(P(None, SUB, None, "colour"), P(None, SUB, None, "colour"), P()),
        check_vma=False,
    )
```

time: 564 us -> 365 us (0.65)
  other arithmetic: 156 us -> 8.58 us
  blocking collectives: 139 us -> 0 us
  waiting for transfers between devices: 169 us -> 37.2 us
  Pallas kernels: 0 us -> 115 us
  starting transfers between devices: 73.2 us -> 161 us
  local copies, waits for them, and re-layouts: 9.26 us -> 35.5 us
  between operations: 7.25 us -> 1.33 us
    ppermute x34 -> x45, waiting for transfers between devices: 169 us -> 37.2 us  [the longest x18 14.7 us: everywhere(): lax.ppermute(value, axis, [(i, i ^ mask) for i in range(count)])]
    pallas_call x0 -> x11, Pallas kernels: none -> 115 us  [the longest x3 52.7 us: second_solve(): pl.pallas_call(functools.partial(second_kernel, r), out_shape=[shape_of()...]
    all_to_all x4 -> x0, blocking collectives: 110 us -> none  [from_everyone(): return lax.all_to_all(copies, axis, split_axis=0, concat_axis=0, tiled=True)]
    ppermute x34 -> x45, starting transfers between devices: 73.2 us -> 161 us  [the longest x18 108 us: everywhere(): lax.ppermute(value, axis, [(i, i ^ mask) for i in range(count)])]
    mul x29 -> x0, other arithmetic: 71.1 us -> none  [the longest x28 69.5 us: jacobi(): found = (found + scale * (resid - (6.0 + diag) * found + beside)) * mask]
    unnamed x66 -> x100, local copies, waits for them, and re-layouts: 1.25 us -> 30.8 us
    psum x4 -> x0, blocking collectives: 29.1 us -> none  [by_axis(): shard = lax.psum(shard, axis)]
    reduce_sum x9 -> x0, other arithmetic: 17.7 us -> none  [the longest x4 15.4 us: colour_step(): upper_part = jnp.sum(resid * correction, axis=(1, 2, 3))]
  transfers between devices with their start and end apart: 34 -> 45, of which waited for: 28 -> 15; matrix products, arithmetic and copies ran while one was open for 10% -> 2% of each run, Pallas kernels for 0% -> 29%
where the time goes in v1:
time: 365 us; the launch traced here: 359 us
  starting transfers between devices  161 us (44%)
  Pallas kernels  115 us (32%)
  waiting for transfers between devices  37.2 us (10%)
  local copies, waits for them, and re-layouts  35.5 us (10%)
  other arithmetic  8.58 us (2%)
    ppermute x18, starting transfers between devices, everywhere(): lax.ppermute(value, axis, [(i, i ^ mask) for i in range(count)])  108 us
    pallas_call x3, Pallas kernels, second_solve(): pl.pallas_call(functools.partial(second_kernel, r), out_shape=[shape_of()...  52.7 us
    pallas_call x3, Pallas kernels, first_solve(): pl.pallas_call(first_kernel, out_shape=[shape_of(), shape_of(3), shape_of...  50.1 us
    ppermute x10, starting transfers between devices, right(): return lax.ppermute(value, SUB, forward)  35.6 us
    unnamed x100, local copies, waits for them, and re-layouts  30.8 us
    ppermute x13, starting transfers between devices, left(): return lax.ppermute(value, SUB, backward)  16.8 us
    ppermute x18, waiting for transfers between devices, everywhere(): lax.ppermute(value, axis, [(i, i ^ mask) for i in range(count)])  14.7 us
    ppermute x13, waiting for transfers between devices, left(): return lax.ppermute(value, SUB, backward)  13.7 us
  transfers between devices with their start and end apart: 45, of which 15 were waited for; matrix products, arithmetic and copies ran while one was open for 2% of the time, Pallas kernels for 29%

profile of v1, /device:TPU:0, one launch (start us, length us, event | category | flops | bytes accessed | tf_op | source)
XLA Modules:
  0.0 358.9 jit_solution(2605907932088664432)
XLA Ops:
  0.7 2.8 copy-done
  3.5 1.6 copy-done.1
  5.1 1.5 shard_map.49
  6.6 3.5 collective-permute-start.1
  10.1 3.4 collective-permute-start.3
  13.5 3.1 collective-permute-start.2
  16.6 3.4 collective-permute-start
  20.0 1.5 shard_map.50
  21.5 2.3 collective-permute-done.3.qh
  23.8 16.7 %shard_map.53 = (f32[18,8,512]{2,1,0:T(8,128)S(1)}, f32[3,18,8,512]{3,2,1,0:T(8,128)S(1)}, f32[2,18,8,512]{3,2,1,0:T(8,128)S(1)}, f32[2,18,8,512]{3,2,1,0:T(8,128)S(1)}, f32[2,8,128]{2,1,0:T(8,128)S(1)}) custom-call(s32[3]{0:T(128)S(1)} %pad_add_fusion.at.where, f32[18,8,512]{2,1,0:T(8,128)S(1)} %collective-permute-done.3.qh, ...), custom_call_target="tpu_custom_call" | custom-call | flops 26542080 | bytes 4718592 | tf_op jit(solution)/shard_map/pallas_call | solution.py:245
  41.8 16.7 %shard_map.52 = (f32[18,8,512]{2,1,0:T(8,128)S(1)}, f32[3,18,8,512]{3,2,1,0:T(8,128)S(1)}, f32[2,18,8,512]{3,2,1,0:T(8,128)S(1)}, f32[2,18,8,512]{3,2,1,0:T(8,128)S(1)}, f32[2,8,128]{2,1,0:T(8,128)S(1)}) custom-call(s32[3]{0:T(128)S(1)} %pad_add_fusion.at.where, f32[18,8,512]{2,1,0:T(8,128)S(1)} %collective-permute-done.2.qh, ...), custom_call_target="tpu_custom_call" | custom-call | flops 26542080 | bytes 4718592 | tf_op jit(solution)/shard_map/pallas_call | solution.py:245
  59.9 16.7 %shard_map.51 = (f32[18,8,512]{2,1,0:T(8,128)S(1)}, f32[3,18,8,512]{3,2,1,0:T(8,128)S(1)}, f32[2,18,8,512]{3,2,1,0:T(8,128)S(1)}, f32[2,18,8,512]{3,2,1,0:T(8,128)S(1)}, f32[2,8,128]{2,1,0:T(8,128)S(1)}) custom-call(s32[3]{0:T(128)S(1)} %pad_add_fusion.at.where, f32[18,8,512]{2,1,0:T(8,128)S(1)} %collective-permute-done.qh, ...), custom_call_target="tpu_custom_call" | custom-call | flops 26542080 | bytes 4718592 | tf_op jit(solution)/shard_map/pallas_call | solution.py:245
  77.9 9.3 %collective-permute-done.4.refs_3_.cr = f32[18,8,512]{2,1,0:T(8,128)S(1)} collective-permute-done((f32[18,8,512]{2,1,0:T(8,128)S(1)}, f32[18,8,512]{2,1,0:T(8,128)S(1)}, u32[]{:S(2)}, u32[]{:S(2)}) %collective-permute-start.4) | collective-permute-done | bytes 294944 | tf_op jit(solution)/shard_map/ppermute | solution.py:533
  89.5 6.4 %collective-permute-start.10 = (f32[8,128]{1,0:T(8,128)S(1)}, f32[8,128]{1,0:T(8,128)S(1)}, u32[]{:S(2)}, u32[]{:S(2)}) collective-permute-start(f32[8,128]{1,0:T(8,128)S(1)} %add.78), channel_id=1, source_target_pairs={{0,3},{1,2},{2,1},{3,0},{4,7},{5,6},{6,5},{7,4},{8,11},{9,10},{10,... | collective-permute-start | bytes 12296 | tf_op jit(solution)/shard_map/ppermute | solution.py:515
  95.9 1.5 collective-permute-start.9
  101.3 6.6 %collective-permute-start.11 = (f32[8,128]{1,0:T(8,128)S(1)}, f32[8,128]{1,0:T(8,128)S(1)}, u32[]{:S(2)}, u32[]{:S(2)}) collective-permute-start(f32[8,128]{1,0:T(8,128)S(1)} %add_add_fusion.5), channel_id=1, source_target_pairs={{0,4},{4,0},{8,12},{12,8},{1,5},{5,1},{9,13},{13,9},{2,6},{6,2},{1... | collective-permute-start | bytes 12296 | tf_op jit(solution)/shard_map/ppermute | solution.py:515
  108.0 3.2 collective-permute-start.12
  111.2 2.1 collective-permute-start.13
  114.6 1.4 collective-permute-done.13
  117.3 53.8 %collective-permute-start.14 = (f32[8,128]{1,0:T(8,128)S(1)}, f32[8,128]{1,0:T(8,128)S(1)}, u32[]{:S(2)}, u32[]{:S(2)}) collective-permute-start(f32[8,128]{1,0:T(8,128)S(1)} %add_add_fusion.4), channel_id=1, source_target_pairs={{0,16},{16,0},{32,48},{48,32},{1,17},{17,1},{33,49},{49,33},{2,18}... | collective-permute-start | bytes 12296 | tf_op jit(solution)/shard_map/ppermute | solution.py:515
  171.1 1.6 collective-permute-done.14
  173.9 2.3 collective-permute-done.15
  178.9 17.5 %shard_map.57 = (f32[18,8,512]{2,1,0:T(8,128)S(1)}, f32[2,18,8,512]{3,2,1,0:T(8,128)S(1)}, f32[18,8,512]{2,1,0:T(8,128)S(1)}, f32[18,8,512]{2,1,0:T(8,128)S(1)},...) custom-call(s32[3]{0:T(128)S(1)} %pad_add_fusion.at.where, ...), custom_call_target="tpu_custom_call" | custom-call | flops 26542080 | bytes 8257536 | tf_op jit(solution)/shard_map/pallas_call | solution.py:366
  197.2 5.2 %collective-permute-start.28 = (f32[18,8,512]{2,1,0:T(8,128)S(1)}, f32[18,8,512]{2,1,0:T(8,128)S(1)}, u32[]{:S(2)}, u32[]{:S(2)}) collective-permute-start(f32[18,8,512]{2,1,0:T(8,128)S(1)} %get-tuple-element.106.refs_22_), channel_id=1, source_target_pairs={{0,1},{1,2},{2,3},{3,4},{4,5},{5,6},{6,7},{7,8},{8,9},{9,10},{10,1... | collective-permute-start | bytes 884744 | tf_op jit(solution)/shard_map/ppermute | solution.py:530
  203.8 17.6 %shard_map.56 = (f32[18,8,512]{2,1,0:T(8,128)S(1)}, f32[2,18,8,512]{3,2,1,0:T(8,128)S(1)}, f32[18,8,512]{2,1,0:T(8,128)S(1)}, f32[18,8,512]{2,1,0:T(8,128)S(1)},...) custom-call(s32[3]{0:T(128)S(1)} %pad_add_fusion.at.where, ...), custom_call_target="tpu_custom_call" | custom-call | flops 26542080 | bytes 8257536 | tf_op jit(solution)/shard_map/pallas_call | solution.py:366
  222.2 4.6 %collective-permute-start.24 = (f32[18,8,512]{2,1,0:T(8,128)S(1)}, f32[18,8,512]{2,1,0:T(8,128)S(1)}, u32[]{:S(2)}, u32[]{:S(2)}) collective-permute-start(f32[18,8,512]{2,1,0:T(8,128)S(1)} %get-tuple-element.98.refs_12_), channel_id=1, source_target_pairs={{0,1},{1,2},{2,3},{3,4},{4,5},{5,6},{6,7},{7,8},{8,9},{9,10},{10,1... | collective-permute-start | bytes 884744 | tf_op jit(solution)/shard_map/ppermute | solution.py:530
  228.1 17.6 %shard_map.55 = (f32[18,8,512]{2,1,0:T(8,128)S(1)}, f32[2,18,8,512]{3,2,1,0:T(8,128)S(1)}, f32[18,8,512]{2,1,0:T(8,128)S(1)}, f32[18,8,512]{2,1,0:T(8,128)S(1)},...) custom-call(s32[3]{0:T(128)S(1)} %pad_add_fusion.at.where, ...), custom_call_target="tpu_custom_call" | custom-call | flops 26542080 | bytes 8257536 | tf_op jit(solution)/shard_map/pallas_call | solution.py:366
  247.4 4.6 %collective-permute-start.20 = (f32[18,8,512]{2,1,0:T(8,128)S(1)}, f32[18,8,512]{2,1,0:T(8,128)S(1)}, u32[]{:S(2)}, u32[]{:S(2)}) collective-permute-start(f32[18,8,512]{2,1,0:T(8,128)S(1)} %get-tuple-element.90.refs_2_), channel_id=1, source_target_pairs={{0,1},{1,2},{2,3},{3,4},{4,5},{5,6},{6,7},{7,8},{8,9},{9,10},{10,1... | collective-permute-start | bytes 884744 | tf_op jit(solution)/shard_map/ppermute | solution.py:530
  253.3 2.8 collective-permute-done.20.refs_5_
  256.1 4.4 %collective-permute-done.21.refs_6_ = f32[18,8,512]{2,1,0:T(8,128)S(1)} collective-permute-done((f32[18,8,512]{2,1,0:T(8,128)S(1)}, f32[18,8,512]{2,1,0:T(8,128)S(1)}, u32[]{:S(2)}, u32[]{:S(2)}) %collective-permute-start.21) | collective-permute-done | bytes 294944 | tf_op jit(solution)/shard_map/ppermute | solution.py:533
  260.6 2.8 shard_map.58
  264.8 2.1 collective-permute-start.31
  266.9 8.3 %collective-permute-start.32 = (f32[16,128]{1,0:T(8,128)S(1)}, f32[16,128]{1,0:T(8,128)S(1)}, u32[]{:S(2)}, u32[]{:S(2)}) collective-permute-start(f32[16,128]{1,0:T(8,128)S(1)} %add.88), channel_id=1, source_target_pairs={{0,2},{1,3},{2,0},{3,1},{4,6},{5,7},{6,4},{7,5},{8,10},{9,11},{10,... | collective-permute-start | bytes 24584 | tf_op jit(solution)/shard_map/ppermute | solution.py:515
  275.2 1.7 collective-permute-done.32
  276.9 3.1 collective-permute-done.33
  280.0 1.8 collective-permute-start.34
  281.8 8.5 %collective-permute-start.35 = (f32[16,128]{1,0:T(8,128)S(1)}, f32[16,128]{1,0:T(8,128)S(1)}, u32[]{:S(2)}, u32[]{:S(2)}) collective-permute-start(f32[16,128]{1,0:T(8,128)S(1)} %add_add_fusion.2), channel_id=1, source_target_pairs={{0,8},{4,12},{8,0},{12,4},{1,9},{5,13},{9,1},{13,5},{2,10},{6,14},... | collective-permute-start | bytes 24584 | tf_op jit(solution)/shard_map/ppermute | solution.py:515
  290.3 2.0 collective-permute-start.42
  292.3 2.9 collective-permute-start.41
  295.2 3.0 collective-permute-start.40
  299.2 2.8 collective-permute-done.37
  302.5 11.7 %collective-permute-start.39 = (f32[16,128]{1,0:T(8,128)S(1)}, f32[16,128]{1,0:T(8,128)}, u32[]{:S(2)}, u32[]{:S(2)}) collective-permute-start(f32[16,128]{1,0:T(8,128)S(1)} %add_add_fusion.1), channel_id=1, source_target_pairs={{0,48},{16,32},{32,16},{48,0},{1,49},{17,33},{33,17},{49,1},{2,50}... | collective-permute-start | bytes 24584 | tf_op jit(solution)/shard_map/ppermute | solution.py:515
  339.1 5.5 %shard_map.59 = (f32[8,128]{1,0:T(8,128)S(1)}, f32[2,3,4,128,256]{4,3,2,1,0:T(8,128)}, f32[2,3,4,128,256]{4,3,2,1,0:T(8,128)}) custom-call(s32[3]{0:T(128)S(1)} %pad_add_fusion.at.where, f32[8,128]{1,0:T(8,128)S(1)} %add_add_fusion.3.table, f32[16,128]{1,0:T(8,128)S(1)} %add_add_fusion.after, f32[18,8,512]{2,1,0:T(8,128)S(1)} %get-tuple-element.62.q0.refs_7_.refs_0_, ...), custom_call_target="tpu_custom_call" | custom-call | flops 8847360 | bytes 20643840 | tf_op jit(solution)/shard_map/pallas_call | solution.py:496
  344.6 2.8 dynamic-slice_bitcast_fusion
  351.2 2.1 bitcast_select_fusion.1
  353.3 1.9 pad_maximum_fusion.1
  355.2 1.9 bitcast_select_fusion.3
  357.1 1.9 pad_maximum_fusion
  (169 shorter events, 55.3 us)
Async XLA Ops:
  6.6 14.9 %collective-permute-start.1 = (f32[18,8,512]{2,1,0:T(8,128)S(1)}, f32[18,8,512]{2,1,0:T(8,128)S(1)}, u32[]{:S(2)}, u32[]{:S(2)}) collective-permute-start(f32[18,8,512]{2,1,0:T(8,128)S(1)} %get-tuple-element.65.d3), channel_id=1, source_target_pairs={{0,1},{1,2},{2,3},{3,4},{4,5},{5,6},{6,7},{7,8},{8,9},{9,10},{10,1... | collective-permute-start | bytes 884744 | tf_op jit(solution)/shard_map/ppermute | solution.py:530
  10.1 13.7 %collective-permute-start.3 = (f32[18,8,512]{2,1,0:T(8,128)S(1)}, f32[18,8,512]{2,1,0:T(8,128)S(1)}, u32[]{:S(2)}, u32[]{:S(2)}) collective-permute-start(f32[18,8,512]{2,1,0:T(8,128)S(1)} %get-tuple-element.75.q3), channel_id=1, source_target_pairs={{0,1},{1,2},{2,3},{3,4},{4,5},{5,6},{6,7},{7,8},{8,9},{9,10},{10,1... | collective-permute-start | bytes 884744 | tf_op jit(solution)/shard_map/ppermute | solution.py:530
  13.5 28.3 %collective-permute-start.2 = (f32[18,8,512]{2,1,0:T(8,128)S(1)}, f32[18,8,512]{2,1,0:T(8,128)S(1)}, u32[]{:S(2)}, u32[]{:S(2)}) collective-permute-start(f32[18,8,512]{2,1,0:T(8,128)S(1)} %get-tuple-element.70.q3), channel_id=1, source_target_pairs={{0,1},{1,2},{2,3},{3,4},{4,5},{5,6},{6,7},{7,8},{8,9},{9,10},{10,1... | collective-permute-start | bytes 884744 | tf_op jit(solution)/shard_map/ppermute | solution.py:530
  16.6 43.2 %collective-permute-start = (f32[18,8,512]{2,1,0:T(8,128)S(1)}, f32[18,8,512]{2,1,0:T(8,128)S(1)}, u32[]{:S(2)}, u32[]{:S(2)}) collective-permute-start(f32[18,8,512]{2,1,0:T(8,128)S(1)} %get-tuple-element.61.q3), channel_id=1, source_target_pairs={{0,1},{1,2},{2,3},{3,4},{4,5},{5,6},{6,7},{7,8},{8,9},{9,10},{10,1... | collective-permute-start | bytes 884744 | tf_op jit(solution)/shard_map/ppermute | solution.py:530
  40.5 220.1 %copy-start.12 = (f32[2,18,8,512]{3,2,1,0:T(8,128)}, f32[2,18,8,512]{3,2,1,0:T(8,128)S(1)}, u32[]{:S(2)}) copy-start(f32[2,18,8,512]{3,2,1,0:T(8,128)S(1)} %get-tuple-element.102.refs_28_.refs_23_) | copy-start | bytes 1769476
  40.5 37.4 %collective-permute-start.6 = (f32[18,8,512]{2,1,0:T(8,128)S(1)}, f32[18,8,512]{2,1,0:T(8,128)S(1)}, u32[]{:S(2)}, u32[]{:S(2)}) collective-permute-start(f32[18,8,512]{2,1,0:T(8,128)S(1)} %get-tuple-element.82), channel_id=1, source_target_pairs={{1,0},{2,1},{3,2},{4,3},{5,4},{6,5},{7,6},{8,7},{9,8},{10,9},{11,1... | collective-permute-start | bytes 884744 | tf_op jit(solution)/shard_map/ppermute | solution.py:533
  58.5 202.1 %copy-start.14 = (f32[2,18,8,512]{3,2,1,0:T(8,128)}, f32[2,18,8,512]{3,2,1,0:T(8,128)S(1)}, u32[]{:S(2)}) copy-start(f32[2,18,8,512]{3,2,1,0:T(8,128)S(1)} %get-tuple-element.94.refs_18_.refs_12_) | copy-start | bytes 1769476
  58.5 19.4 %collective-permute-start.5 = (f32[18,8,512]{2,1,0:T(8,128)S(1)}, f32[18,8,512]{2,1,0:T(8,128)S(1)}, u32[]{:S(2)}, u32[]{:S(2)}) collective-permute-start(f32[18,8,512]{2,1,0:T(8,128)S(1)} %get-tuple-element.81), channel_id=1, source_target_pairs={{1,0},{2,1},{3,2},{4,3},{5,4},{6,5},{7,6},{8,7},{9,8},{10,9},{11,1... | collective-permute-start | bytes 884744 | tf_op jit(solution)/shard_map/ppermute | solution.py:533
  76.6 184.0 %copy-start.16 = (f32[2,18,8,512]{3,2,1,0:T(8,128)}, f32[2,18,8,512]{3,2,1,0:T(8,128)S(1)}, u32[]{:S(2)}) copy-start(f32[2,18,8,512]{3,2,1,0:T(8,128)S(1)} %get-tuple-element.86.refs_8_.refs_1_) | copy-start | bytes 1769476
  76.6 10.6 %collective-permute-start.4 = (f32[18,8,512]{2,1,0:T(8,128)S(1)}, f32[18,8,512]{2,1,0:T(8,128)S(1)}, u32[]{:S(2)}, u32[]{:S(2)}) collective-permute-start(f32[18,8,512]{2,1,0:T(8,128)S(1)} %get-tuple-element.80), channel_id=1, source_target_pairs={{1,0},{2,1},{3,2},{4,3},{5,4},{6,5},{7,6},{8,7},{9,8},{10,9},{11,1... | collective-permute-start | bytes 884744 | tf_op jit(solution)/shard_map/ppermute | solution.py:533
  88.3 1.2 collective-permute-start.7
  89.5 10.5 %collective-permute-start.10 = (f32[8,128]{1,0:T(8,128)S(1)}, f32[8,128]{1,0:T(8,128)S(1)}, u32[]{:S(2)}, u32[]{:S(2)}) collective-permute-start(f32[8,128]{1,0:T(8,128)S(1)} %add.78), channel_id=1, source_target_pairs={{0,3},{1,2},{2,1},{3,0},{4,7},{5,6},{6,5},{7,4},{8,11},{9,10},{10,... | collective-permute-start | bytes 12296 | tf_op jit(solution)/shard_map/ppermute | solution.py:515
  95.9 5.4 %collective-permute-start.8 = (f32[8,128]{1,0:T(8,128)S(1)}, f32[8,128]{1,0:T(8,128)S(1)}, u32[]{:S(2)}, u32[]{:S(2)}) collective-permute-start(f32[8,128]{1,0:T(8,128)S(1)} %add.78), channel_id=1, source_target_pairs={{0,1},{1,0},{2,3},{3,2},{4,5},{5,4},{6,7},{7,6},{8,9},{9,8},{10,11... | collective-permute-start | bytes 12296 | tf_op jit(solution)/shard_map/ppermute | solution.py:515
  95.9 5.4 %collective-permute-start.9 = (f32[8,128]{1,0:T(8,128)S(1)}, f32[8,128]{1,0:T(8,128)S(1)}, u32[]{:S(2)}, u32[]{:S(2)}) collective-permute-start(f32[8,128]{1,0:T(8,128)S(1)} %add.78), channel_id=1, source_target_pairs={{0,2},{1,3},{2,0},{3,1},{4,6},{5,7},{6,4},{7,5},{8,10},{9,11},{10,... | collective-permute-start | bytes 12296 | tf_op jit(solution)/shard_map/ppermute | solution.py:515
  97.4 19.9 %collective-permute-start.18 = (f32[18,8,512]{2,1,0:T(8,128)S(1)}, f32[18,8,512]{2,1,0:T(8,128)S(1)}, u32[]{:S(2)}, u32[]{:S(2)}) collective-permute-start(f32[18,8,512]{2,1,0:T(8,128)S(1)} %get-tuple-element.66.d0), channel_id=1, source_target_pairs={{1,0},{2,1},{3,2},{4,3},{5,4},{6,5},{7,6},{8,7},{9,8},{10,9},{11,1... | collective-permute-start | bytes 884744 | tf_op jit(solution)/shard_map/ppermute | solution.py:533
  98.7 72.4 %collective-permute-start.26 = (f32[18,8,512]{2,1,0:T(8,128)S(1)}, f32[18,8,512]{2,1,0:T(8,128)S(1)}, u32[]{:S(2)}, u32[]{:S(2)}) collective-permute-start(f32[18,8,512]{2,1,0:T(8,128)S(1)} %get-tuple-element.76.q0.refs_27_.refs_22_), channel_id=1, source_target_pairs={{1,0},{2,1},{3,2},{4,3},{5,4},{6,5},{7,6},{8,7},{9,8},{10,9},{11,1... | collective-permute-start | bytes 884744 | tf_op jit(solution)/shard_map/ppermute | solution.py:533
  100.0 78.9 %collective-permute-start.27 = (f32[2,18,8,512]{3,2,1,0:T(8,128)S(1)}, f32[2,18,8,512]{3,2,1,0:T(8,128)S(1)}, u32[]{:S(2)}, u32[]{:S(2)}) collective-permute-start(f32[2,18,8,512]{3,2,1,0:T(8,128)S(1)} %get-tuple-element.102.refs_28_.refs_23_), channel_id=1, source_target_pairs={{1,0},{2,1},{3,2},{4,3},{5,4},{6,5},{7,6},{8,7},{9,8},{10,9},{11,1... | collective-permute-start | bytes 1769480 | tf_op jit(solution)/shard_map/ppermute | solution.py:533
  101.3 9.8 %collective-permute-start.11 = (f32[8,128]{1,0:T(8,128)S(1)}, f32[8,128]{1,0:T(8,128)S(1)}, u32[]{:S(2)}, u32[]{:S(2)}) collective-permute-start(f32[8,128]{1,0:T(8,128)S(1)} %add_add_fusion.5), channel_id=1, source_target_pairs={{0,4},{4,0},{8,12},{12,8},{1,5},{5,1},{9,13},{13,9},{2,6},{6,2},{1... | collective-permute-start | bytes 12296 | tf_op jit(solution)/shard_map/ppermute | solution.py:515
  108.0 5.3 %collective-permute-start.12 = (f32[8,128]{1,0:T(8,128)S(1)}, f32[8,128]{1,0:T(8,128)S(1)}, u32[]{:S(2)}, u32[]{:S(2)}) collective-permute-start(f32[8,128]{1,0:T(8,128)S(1)} %add_add_fusion.5), channel_id=1, source_target_pairs={{0,8},{4,12},{8,0},{12,4},{1,9},{5,13},{9,1},{13,5},{2,10},{6,14},... | collective-permute-start | bytes 12296 | tf_op jit(solution)/shard_map/ppermute | solution.py:515
  111.2 4.8 %collective-permute-start.13 = (f32[8,128]{1,0:T(8,128)S(1)}, f32[8,128]{1,0:T(8,128)S(1)}, u32[]{:S(2)}, u32[]{:S(2)}) collective-permute-start(f32[8,128]{1,0:T(8,128)S(1)} %add_add_fusion.5), channel_id=1, source_target_pairs={{0,12},{4,8},{8,4},{12,0},{1,13},{5,9},{9,5},{13,1},{2,14},{6,10},... | collective-permute-start | bytes 12296 | tf_op jit(solution)/shard_map/ppermute | solution.py:515
  113.3 90.4 %collective-permute-start.23 = (f32[2,18,8,512]{3,2,1,0:T(8,128)S(1)}, f32[2,18,8,512]{3,2,1,0:T(8,128)S(1)}, u32[]{:S(2)}, u32[]{:S(2)}) collective-permute-start(f32[2,18,8,512]{3,2,1,0:T(8,128)S(1)} %get-tuple-element.94.refs_18_.refs_12_), channel_id=1, source_target_pairs={{1,0},{2,1},{3,2},{4,3},{5,4},{6,5},{7,6},{8,7},{9,8},{10,9},{11,1... | collective-permute-start | bytes 1769480 | tf_op jit(solution)/shard_map/ppermute | solution.py:533
  116.0 112.1 %collective-permute-start.19 = (f32[2,18,8,512]{3,2,1,0:T(8,128)S(1)}, f32[2,18,8,512]{3,2,1,0:T(8,128)S(1)}, u32[]{:S(2)}, u32[]{:S(2)}) collective-permute-start(f32[2,18,8,512]{3,2,1,0:T(8,128)S(1)} %get-tuple-element.86.refs_8_.refs_1_), channel_id=1, source_target_pairs={{1,0},{2,1},{3,2},{4,3},{5,4},{6,5},{7,6},{8,7},{9,8},{10,9},{11,1... | collective-permute-start | bytes 1769480 | tf_op jit(solution)/shard_map/ppermute | solution.py:533
  117.3 55.4 %collective-permute-start.14 = (f32[8,128]{1,0:T(8,128)S(1)}, f32[8,128]{1,0:T(8,128)S(1)}, u32[]{:S(2)}, u32[]{:S(2)}) collective-permute-start(f32[8,128]{1,0:T(8,128)S(1)} %add_add_fusion.4), channel_id=1, source_target_pairs={{0,16},{16,0},{32,48},{48,32},{1,17},{17,1},{33,49},{49,33},{2,18}... | collective-permute-start | bytes 12296 | tf_op jit(solution)/shard_map/ppermute | solution.py:515
  171.1 5.1 %collective-permute-start.15 = (f32[8,128]{1,0:T(8,128)S(1)}, f32[8,128]{1,0:T(8,128)S(1)}, u32[]{:S(2)}, u32[]{:S(2)}) collective-permute-start(f32[8,128]{1,0:T(8,128)S(1)} %add_add_fusion.4), channel_id=1, source_target_pairs={{0,32},{16,48},{32,0},{48,16},{1,33},{17,49},{33,1},{49,17},{2,34}... | collective-permute-start | bytes 12296 | tf_op jit(solution)/shard_map/ppermute | solution.py:515
  172.7 4.8 %collective-permute-start.16 = (f32[8,128]{1,0:T(8,128)S(1)}, f32[8,128]{1,0:T(8,128)S(1)}, u32[]{:S(2)}, u32[]{:S(2)}) collective-permute-start(f32[8,128]{1,0:T(8,128)S(1)} %add_add_fusion.4), channel_id=1, source_target_pairs={{0,48},{16,32},{32,16},{48,0},{1,49},{17,33},{33,17},{49,1},{2,50}... | collective-permute-start | bytes 12296 | tf_op jit(solution)/shard_map/ppermute | solution.py:515
  176.2 26.2 %collective-permute-start.22 = (f32[18,8,512]{2,1,0:T(8,128)S(1)}, f32[18,8,512]{2,1,0:T(8,128)S(1)}, u32[]{:S(2)}, u32[]{:S(2)}) collective-permute-start(f32[18,8,512]{2,1,0:T(8,128)S(1)} %get-tuple-element.71.q0.refs_17_.refs_11_), channel_id=1, source_target_pairs={{1,0},{2,1},{3,2},{4,3},{5,4},{6,5},{7,6},{8,7},{9,8},{10,9},{11,1... | collective-permute-start | bytes 884744 | tf_op jit(solution)/shard_map/ppermute | solution.py:533
  177.5 49.2 %collective-permute-start.17 = (f32[18,8,512]{2,1,0:T(8,128)S(1)}, f32[18,8,512]{2,1,0:T(8,128)S(1)}, u32[]{:S(2)}, u32[]{:S(2)}) collective-permute-start(f32[18,8,512]{2,1,0:T(8,128)S(1)} %get-tuple-element.62.q0.refs_7_.refs_0_), channel_id=1, source_target_pairs={{1,0},{2,1},{3,2},{4,3},{5,4},{6,5},{7,6},{8,7},{9,8},{10,9},{11,1... | collective-permute-start | bytes 884744 | tf_op jit(solution)/shard_map/ppermute | solution.py:533
  197.2 54.7 %collective-permute-start.28 = (f32[18,8,512]{2,1,0:T(8,128)S(1)}, f32[18,8,512]{2,1,0:T(8,128)S(1)}, u32[]{:S(2)}, u32[]{:S(2)}) collective-permute-start(f32[18,8,512]{2,1,0:T(8,128)S(1)} %get-tuple-element.106.refs_22_), channel_id=1, source_target_pairs={{0,1},{1,2},{2,3},{3,4},{4,5},{5,6},{6,7},{7,8},{8,9},{9,10},{10,1... | collective-permute-start | bytes 884744 | tf_op jit(solution)/shard_map/ppermute | solution.py:530
  202.5 50.8 %collective-permute-start.29 = (f32[18,8,512]{2,1,0:T(8,128)S(1)}, f32[18,8,512]{2,1,0:T(8,128)S(1)}, u32[]{:S(2)}, u32[]{:S(2)}) collective-permute-start(f32[18,8,512]{2,1,0:T(8,128)S(1)} %get-tuple-element.105.refs_21_.refs_28_), channel_id=1, source_target_pairs={{1,0},{2,1},{3,2},{4,3},{5,4},{6,5},{7,6},{8,7},{9,8},{10,9},{11,1... | collective-permute-start | bytes 884744 | tf_op jit(solution)/shard_map/ppermute | solution.py:533
  222.2 31.1 %collective-permute-start.24 = (f32[18,8,512]{2,1,0:T(8,128)S(1)}, f32[18,8,512]{2,1,0:T(8,128)S(1)}, u32[]{:S(2)}, u32[]{:S(2)}) collective-permute-start(f32[18,8,512]{2,1,0:T(8,128)S(1)} %get-tuple-element.98.refs_12_), channel_id=1, source_target_pairs={{0,1},{1,2},{2,3},{3,4},{4,5},{5,6},{6,7},{7,8},{8,9},{9,10},{10,1... | collective-permute-start | bytes 884744 | tf_op jit(solution)/shard_map/ppermute | solution.py:530
  226.8 26.5 %collective-permute-start.25 = (f32[18,8,512]{2,1,0:T(8,128)S(1)}, f32[18,8,512]{2,1,0:T(8,128)S(1)}, u32[]{:S(2)}, u32[]{:S(2)}) collective-permute-start(f32[18,8,512]{2,1,0:T(8,128)S(1)} %get-tuple-element.97.refs_11_.refs_17_), channel_id=1, source_target_pairs={{1,0},{2,1},{3,2},{4,3},{5,4},{6,5},{7,6},{8,7},{9,8},{10,9},{11,1... | collective-permute-start | bytes 884744 | tf_op jit(solution)/shard_map/ppermute | solution.py:533
  247.4 8.8 %collective-permute-start.20 = (f32[18,8,512]{2,1,0:T(8,128)S(1)}, f32[18,8,512]{2,1,0:T(8,128)S(1)}, u32[]{:S(2)}, u32[]{:S(2)}) collective-permute-start(f32[18,8,512]{2,1,0:T(8,128)S(1)} %get-tuple-element.90.refs_2_), channel_id=1, source_target_pairs={{0,1},{1,2},{2,3},{3,4},{4,5},{5,6},{6,7},{7,8},{8,9},{9,10},{10,1... | collective-permute-start | bytes 884744 | tf_op jit(solution)/shard_map/ppermute | solution.py:530
  252.0 8.6 %collective-permute-start.21 = (f32[18,8,512]{2,1,0:T(8,128)S(1)}, f32[18,8,512]{2,1,0:T(8,128)S(1)}, u32[]{:S(2)}, u32[]{:S(2)}) collective-permute-start(f32[18,8,512]{2,1,0:T(8,128)S(1)} %get-tuple-element.89.refs_1_.refs_6_), channel_id=1, source_target_pairs={{1,0},{2,1},{3,2},{4,3},{5,4},{6,5},{7,6},{8,7},{9,8},{10,9},{11,1... | collective-permute-start | bytes 884744 | tf_op jit(solution)/shard_map/ppermute | solution.py:533
  263.6 1.3 collective-permute-start.30
  264.8 10.4 %collective-permute-start.31 = (f32[16,128]{1,0:T(8,128)S(1)}, f32[16,128]{1,0:T(8,128)S(1)}, u32[]{:S(2)}, u32[]{:S(2)}) collective-permute-start(f32[16,128]{1,0:T(8,128)S(1)} %add.88), channel_id=1, source_target_pairs={{0,1},{1,0},{2,3},{3,2},{4,5},{5,4},{6,7},{7,6},{8,9},{9,8},{10,11... | collective-permute-start | bytes 24584 | tf_op jit(solution)/shard_map/ppermute | solution.py:515
  266.9 10.0 %collective-permute-start.32 = (f32[16,128]{1,0:T(8,128)S(1)}, f32[16,128]{1,0:T(8,128)S(1)}, u32[]{:S(2)}, u32[]{:S(2)}) collective-permute-start(f32[16,128]{1,0:T(8,128)S(1)} %add.88), channel_id=1, source_target_pairs={{0,2},{1,3},{2,0},{3,1},{4,6},{5,7},{6,4},{7,5},{8,10},{9,11},{10,... | collective-permute-start | bytes 24584 | tf_op jit(solution)/shard_map/ppermute | solution.py:515
  275.2 4.9 %collective-permute-start.33 = (f32[16,128]{1,0:T(8,128)S(1)}, f32[16,128]{1,0:T(8,128)S(1)}, u32[]{:S(2)}, u32[]{:S(2)}) collective-permute-start(f32[16,128]{1,0:T(8,128)S(1)} %add.88), channel_id=1, source_target_pairs={{0,3},{1,2},{2,1},{3,0},{4,7},{5,6},{6,5},{7,4},{8,11},{9,10},{10,... | collective-permute-start | bytes 24584 | tf_op jit(solution)/shard_map/ppermute | solution.py:515
  280.0 15.1 %collective-permute-start.34 = (f32[16,128]{1,0:T(8,128)S(1)}, f32[16,128]{1,0:T(8,128)S(1)}, u32[]{:S(2)}, u32[]{:S(2)}) collective-permute-start(f32[16,128]{1,0:T(8,128)S(1)} %add_add_fusion.2), channel_id=1, source_target_pairs={{0,4},{4,0},{8,12},{12,8},{1,5},{5,1},{9,13},{13,9},{2,6},{6,2},{1... | collective-permute-start | bytes 24584 | tf_op jit(solution)/shard_map/ppermute | solution.py:515
  281.8 16.4 %collective-permute-start.35 = (f32[16,128]{1,0:T(8,128)S(1)}, f32[16,128]{1,0:T(8,128)S(1)}, u32[]{:S(2)}, u32[]{:S(2)}) collective-permute-start(f32[16,128]{1,0:T(8,128)S(1)} %add_add_fusion.2), channel_id=1, source_target_pairs={{0,8},{4,12},{8,0},{12,4},{1,9},{5,13},{9,1},{13,5},{2,10},{6,14},... | collective-permute-start | bytes 24584 | tf_op jit(solution)/shard_map/ppermute | solution.py:515
  290.3 7.9 %collective-permute-start.36 = (f32[16,128]{1,0:T(8,128)S(1)}, f32[16,128]{1,0:T(8,128)S(1)}, u32[]{:S(2)}, u32[]{:S(2)}) collective-permute-start(f32[16,128]{1,0:T(8,128)S(1)} %add_add_fusion.2), channel_id=1, source_target_pairs={{0,12},{4,8},{8,4},{12,0},{1,13},{5,9},{9,5},{13,1},{2,14},{6,10},... | collective-permute-start | bytes 24584 | tf_op jit(solution)/shard_map/ppermute | solution.py:515
  290.3 26.4 %collective-permute-start.42 = (f32[18,8,512]{2,1,0:T(8,128)}, f32[18,8,512]{2,1,0:T(8,128)}, u32[]{:S(2)}, u32[]{:S(2)}) collective-permute-start(f32[18,8,512]{2,1,0:T(8,128)} %get-tuple-element.108.refs_24_), channel_id=1, source_target_pairs={{0,1},{1,2},{2,3},{3,4},{4,5},{5,6},{6,7},{7,8},{8,9},{9,10},{10,1... | collective-permute-start | bytes 884744 | tf_op jit(solution)/shard_map/ppermute | solution.py:530
  292.3 24.4 %collective-permute-start.41 = (f32[18,8,512]{2,1,0:T(8,128)}, f32[18,8,512]{2,1,0:T(8,128)}, u32[]{:S(2)}, u32[]{:S(2)}) collective-permute-start(f32[18,8,512]{2,1,0:T(8,128)} %get-tuple-element.100.refs_14_), channel_id=1, source_target_pairs={{0,1},{1,2},{2,3},{3,4},{4,5},{5,6},{6,7},{7,8},{8,9},{9,10},{10,1... | collective-permute-start | bytes 884744 | tf_op jit(solution)/shard_map/ppermute | solution.py:530
  295.2 21.5 %collective-permute-start.40 = (f32[18,8,512]{2,1,0:T(8,128)}, f32[18,8,512]{2,1,0:T(8,128)}, u32[]{:S(2)}, u32[]{:S(2)}) collective-permute-start(f32[18,8,512]{2,1,0:T(8,128)} %get-tuple-element.92.refs_4_), channel_id=1, source_target_pairs={{0,1},{1,2},{2,3},{3,4},{4,5},{5,6},{6,7},{7,8},{8,9},{9,10},{10,1... | collective-permute-start | bytes 884744 | tf_op jit(solution)/shard_map/ppermute | solution.py:530
  298.2 3.7 %collective-permute-start.37 = (f32[16,128]{1,0:T(8,128)S(1)}, f32[16,128]{1,0:T(8,128)S(1)}, u32[]{:S(2)}, u32[]{:S(2)}) collective-permute-start(f32[16,128]{1,0:T(8,128)S(1)} %add_add_fusion.1), channel_id=1, source_target_pairs={{0,16},{16,0},{32,48},{48,32},{1,17},{17,1},{33,49},{49,33},{2,18}... | collective-permute-start | bytes 24584 | tf_op jit(solution)/shard_map/ppermute | solution.py:515
  298.4 16.4 %collective-permute-start.38 = (f32[16,128]{1,0:T(8,128)S(1)}, f32[16,128]{1,0:T(8,128)}, u32[]{:S(2)}, u32[]{:S(2)}) collective-permute-start(f32[16,128]{1,0:T(8,128)S(1)} %add_add_fusion.1), channel_id=1, source_target_pairs={{0,32},{16,48},{32,0},{48,16},{1,33},{17,49},{33,1},{49,17},{2,34}... | collective-permute-start | bytes 24584 | tf_op jit(solution)/shard_map/ppermute | solution.py:515
  302.5 13.4 %collective-permute-start.39 = (f32[16,128]{1,0:T(8,128)S(1)}, f32[16,128]{1,0:T(8,128)}, u32[]{:S(2)}, u32[]{:S(2)}) collective-permute-start(f32[16,128]{1,0:T(8,128)S(1)} %add_add_fusion.1), channel_id=1, source_target_pairs={{0,48},{16,32},{32,16},{48,0},{1,49},{17,33},{33,17},{49,1},{2,50}... | collective-permute-start | bytes 24584 | tf_op jit(solution)/shard_map/ppermute | solution.py:515
  347.4 3.8 %collective-permute-start.44 = (f32[3,4,128,256]{3,2,1,0:T(8,128)}, f32[3,4,128,256]{3,2,1,0:T(8,128)}, u32[]{:S(2)}, u32[]{:S(2)}) collective-permute-start(f32[3,4,128,256]{3,2,1,0:T(8,128)} %dynamic-slice_bitcast_fusion), channel_id=1, source_target_pairs={{0,64},{64,0},{1,65},{65,1},{2,66},{66,2},{3,67},{67,3},{4,68},{68... | collective-permute-start | bytes 4718600 | tf_op jit(solution)/shard_map/ppermute | solution.py:577
  348.7 6.5 %collective-permute-start.43 = (f32[3,4,128,256]{3,2,1,0:T(8,128)}, f32[3,4,128,256]{3,2,1,0:T(8,128)}, u32[]{:S(2)}, u32[]{:S(2)}) collective-permute-start(f32[3,4,128,256]{3,2,1,0:T(8,128)} %dynamic-slice_bitcast_fusion.1), channel_id=1, source_target_pairs={{0,64},{64,0},{1,65},{65,1},{2,66},{66,2},{3,67},{67,3},{4,68},{68... | collective-permute-start | bytes 4718600 | tf_op jit(solution)/shard_map/ppermute | solution.py:577
  (47 other events, 831.9 us)
